TPU v7x, 512 devices: a whole 4x4x16 slice. The times are simulated.
512 devices in a mesh: gx: 64 (over y, x, z_hi, core), gy: 8 (over z_lo).
Axes of the slice: x: 4, y: 4, z: 16 (z_hi: 2, z_lo: 8; z = z_hi * 8 + z_lo), core: 2. Of those that a mesh axis runs over, the one named last changes fastest.
Arguments:
- adjoint_init: float32 [3, 512, 64, 256], P(None, 'gx', 'gy'), may hold values from -6 to 6
- saved_states: bfloat16 [4, 3, 512, 64, 256], P(None, None, 'gx', 'gy'), may hold values from -4 to 4
- step_index: int32 [4], replicated, may hold values from 0 to 3
- vertical_inverse: float32 [256, 256], replicated, may hold values from -1 to 2
- disk_filter: bfloat16 [64, 8, 8, 64, 512], P('gx', 'gy'), may hold values from -0.25 to 0.25
- pair_turbine: int32 [64, 8, 8], P('gx', 'gy'), may hold values from 0 to 96, as said below
- pair_tile: int32 [64, 8, 8], P('gx', 'gy'), may hold values from 0 to 31
- turbine_owner: int32 [96], replicated, may hold values from 0 to 511
Outputs:
- adjoint_final: float32 [3, 512, 64, 256], P(None, 'gx', 'gy')
- turbine_grad: float32 [64, 8, 96], P('gx', 'gy')
Inputs may be any that keep to these rules, and one draw needn't show every extreme that they name: `pair_turbine`: entry 96 marks an empty slot.
All inputs are finite; a program needn't handle non-finite values.
Results may differ from a plain program's by a relative error of at most 0.0024.
Values may be sent and summed in bfloat16 or wider, within the bound.
No kernel may reach another device: no remote copies, remote signals or barrier semaphores. Data moves between devices by JAX's collectives and lax.ppermute only.
A program may use at most 64 MiB of HBM per device.

v0:
```python
import functools

import jax
import jax.numpy as jnp
from jax import lax
from jax.sharding import Mesh
from jax.sharding import PartitionSpec as P

STEPS = 4
GX_GY = ("gx_0", "gx_1", "gx_2", "gx_3", "gy")
GX = ("gx_0", "gx_1", "gx_2", "gx_3")


COURANT = 0.2


def padded_2(x, sides, width):
    edges = {}
    for axis, dim in sides:
        devices, length = (lax.axis_size(axis), x.shape[dim])
        up = [(i, (i + 1) % devices) for i in range(devices)]
        last = lax.slice_in_dim(x, length - width, length, axis=dim)
        initial = lax.slice_in_dim(x, 0, width, axis=dim)
        edges[dim] = (
            lax.ppermute(last, axis, up),
            lax.ppermute(initial, axis, [(b, a) for a, b in up]),
        )
    done = []
    for _, dim in sides:
        low, high = edges[dim]
        around = [(width, width) if d in done else (0, 0) for d in range(x.ndim)]
        x = jnp.concatenate([jnp.pad(low, around), x, jnp.pad(high, around)], axis=dim)
        done.append(dim)
    return x


def over_axes(x, axes):
    return functools.reduce(lax.psum, axes, x)


def vertical_difference(values):
    padded = jnp.pad(values, ((0, 0), (0, 0), (0, 0), (1, 1)))
    return 0.5 * (padded[..., 2:] - padded[..., :-2])


def planar_differences(stream_rim, span_rim):
    return (
        0.5 * (stream_rim[:, 2:] - stream_rim[:, :-2]),
        0.5 * (span_rim[:, :, 2:] - span_rim[:, :, :-2]),
    )


def adjoint_rims(values):
    padded = padded_2(values, ((GX, 1), ("gy", 2)), 1)
    return (padded[:, :, 1:-1], padded[:, 1:-1, :])


def states_rims(values):
    padded = padded_2(values, ((GX, 2), ("gy", 3)), 1)
    return (padded[:, :, :, 1:-1], padded[:, :, 1:-1, :])


def body(
    adjoint_init,
    saved_states,
    step_index,
    vertical_inverse,
    disk_filter,
    pair_turbine,
    pair_tile,
    turbine_owner,
):
    stream_cols = adjoint_init.shape[1]
    span_cols = adjoint_init.shape[2]
    levels = adjoint_init.shape[3]
    turbines = turbine_owner.shape[0]
    tile_rows = stream_cols * span_cols // 2
    filters = disk_filter[0, 0]
    slot_tiles = pair_tile[0, 0]
    matches = (
        pair_turbine[0, 0][:, None] == jnp.arange(turbines, dtype=jnp.int32)[None, :]
    ).astype(jnp.float32)
    adjoint = adjoint_init
    totals = jnp.zeros((turbines,), jnp.float32)
    all_stream_rims, all_span_rims = states_rims(saved_states)
    for number in range(STEPS):
        stored = lax.dynamic_index_in_dim(saved_states, step_index[number], 0, keepdims=False)
        forward_stream_rim = lax.dynamic_index_in_dim(
            all_stream_rims, step_index[number], 0, keepdims=False
        )
        forward_span_rim = lax.dynamic_index_in_dim(
            all_span_rims, step_index[number], 0, keepdims=False
        )
        forward_stream, forward_span = planar_differences(
            forward_stream_rim.astype(jnp.float32), forward_span_rim.astype(jnp.float32)
        )
        velocity = stored.astype(jnp.float32)
        forward_depth = vertical_difference(velocity)
        solved = jnp.dot(
            adjoint.reshape(-1, levels),
            vertical_inverse,
            precision=lax.Precision.HIGHEST,
            preferred_element_type=jnp.float32,
        ).reshape(adjoint.shape)
        solved_stream_rim, solved_span_rim = adjoint_rims(solved)
        solved_stream, solved_span = planar_differences(solved_stream_rim, solved_span_rim)
        solved_depth = vertical_difference(solved)
        advect = (
            velocity[0:1] * solved_stream
            + velocity[1:2] * solved_span
            + velocity[2:3] * solved_depth
        )
        derivs = (forward_stream, forward_span, forward_depth)
        couple = jnp.stack(
            [
                solved[0] * derivs[component][0]
                + solved[1] * derivs[component][1]
                + solved[2] * derivs[component][2]
                for component in range(3)
            ]
        )
        adjoint = solved + COURANT * (advect - couple)
        adjoint_tiles = adjoint[0].astype(jnp.bfloat16).reshape(tile_rows, 2 * levels)
        speed_tiles = stored[0].reshape(tile_rows, 2 * levels)
        picked_adjoint = jnp.take(adjoint_tiles, slot_tiles, axis=0)
        picked_speed = jnp.take(speed_tiles, slot_tiles, axis=0)
        sampled = jnp.einsum(
            "jpt,jt->jp", filters, picked_adjoint, preferred_element_type=jnp.float32
        )
        speeds = jnp.einsum("jpt,jt->jp", filters, picked_speed, preferred_element_type=jnp.float32)
        contribs = jnp.mean(speeds * speeds * sampled, axis=1)
        partial_value = jnp.sum(contribs[:, None] * matches, axis=0)
        totals = totals + over_axes(partial_value, GX_GY)
    own_index = lax.axis_index(GX) * lax.axis_size("gy") + lax.axis_index("gy")
    owned_mask = turbine_owner == own_index
    turbine_grad = jnp.where(owned_mask, totals, jnp.float32(0.0))[None, None, :]
    return (adjoint, turbine_grad)


def solution(mesh):
    torus = Mesh(
        mesh.devices.reshape(4, 4, 2, 2, mesh.shape["gy"]), ("gx_0", "gx_1", "gx_2", "gx_3", "gy")
    )
    placed = (
        P(None, GX, "gy", None),
        P(None, None, GX, "gy", None),
        P(),
        P(),
        P(GX, "gy", None, None, None),
        P(GX, "gy", None),
        P(GX, "gy", None),
        P(),
    )
    return jax.shard_map(
        body,
        mesh=torus,
        in_specs=placed,
        out_specs=(P(None, GX, "gy", None), P(GX, "gy", None)),
        check_vma=False,
    )
```

profile of v0, /device:TPU:1, one launch (start us, length us, event | category | flops | bytes accessed | tf_op | source)
XLA Modules:
  0.0 244.4 jit_solution(881389248281111836)
XLA Ops:
  0.7 0.9 fusion.138
  1.6 8.7 %collective-permute-start.5 = (bf16[4,3,1,8,256]{4,3,2,1,0:T(8,128)(2,1)S(1)}, bf16[4,3,1,8,256]{4,3,2,1,0:T(8,128)(2,1)S(1)}, u32[]{:S(2)}, u32[]{:S(2)}) collective-permute-start(bf16[4,3,1,8,256]{4,3,2,1,0:T(8,128)(2,1)S(1)} %get-tuple-element.29), channel_id=1, source_target_pairs={{8,0},{16,8},{24,16},{32,24},{40,32},{48,40},{56,48},{64,56},{72,6... | collective-permute-start | bytes 147464 | tf_op jit(solution)/shard_map/ppermute | solution.py:26
  10.3 10.0 %collective-permute-start.4 = (bf16[4,3,1,8,256]{4,3,2,1,0:T(8,128)(2,1)S(1)}, bf16[4,3,1,8,256]{4,3,2,1,0:T(8,128)(2,1)S(1)}, u32[]{:S(2)}, u32[]{:S(2)}) collective-permute-start(bf16[4,3,1,8,256]{4,3,2,1,0:T(8,128)(2,1)S(1)} %get-tuple-element.30), channel_id=1, source_target_pairs={{0,8},{8,16},{16,24},{24,32},{32,40},{40,48},{48,56},{56,64},{64,7... | collective-permute-start | bytes 147464 | tf_op jit(solution)/shard_map/ppermute | solution.py:25
  20.3 1.4 fusion.148
  21.7 2.4 collective-permute-start.1
  24.1 5.9 %collective-permute-start = (f32[3,1,8,256]{3,2,1,0:T(8,128)S(1)}, f32[3,1,8,256]{3,2,1,0:T(8,128)S(1)}, u32[]{:S(2)}, u32[]{:S(2)}) collective-permute-start(f32[3,1,8,256]{3,2,1,0:T(8,128)S(1)} %get-tuple-element.70), channel_id=1, source_target_pairs={{8,0},{16,8},{24,16},{32,24},{40,32},{48,40},{56,48},{64,56},{72,6... | collective-permute-start | bytes 73736 | tf_op jit(solution)/shard_map/ppermute | solution.py:26
  30.1 5.4 %collective-permute-start.2 = (f32[3,8,1,256]{3,2,1,0:T(1,128)S(1)}, f32[3,8,1,256]{3,2,1,0:T(1,128)S(1)}, u32[]{:S(2)}, u32[]{:S(2)}) collective-permute-start(f32[3,8,1,256]{3,2,1,0:T(1,128)S(1)} %get-tuple-element.67), channel_id=1, source_target_pairs={{1,0},{2,1},{3,2},{4,3},{5,4},{6,5},{7,6},{0,7},{9,8},{10,9},{11,1... | collective-permute-start | bytes 73736 | tf_op jit(solution)/shard_map/ppermute | solution.py:26
  35.5 0.6 fusion.147
  44.0 0.3 fusion.43
  44.3 0.3 fusion.27
  44.7 0.6 gather_fusion
  45.2 0.6 gather_fusion.6
  45.8 0.6 gather_fusion.4
  46.4 0.6 gather_fusion.2
  47.0 1.9 collective-permute-start.6
  49.0 10.0 %collective-permute-start.7 = (bf16[4,3,8,1,256]{4,3,2,1,0:T(2,128)(2,1)S(1)}, bf16[4,3,8,1,256]{4,3,2,1,0:T(2,128)(2,1)S(1)}, u32[]{:S(2)}, u32[]{:S(2)}) collective-permute-start(bf16[4,3,8,1,256]{4,3,2,1,0:T(2,128)(2,1)S(1)} %get-tuple-element.28), channel_id=1, source_target_pairs={{1,0},{2,1},{3,2},{4,3},{5,4},{6,5},{7,6},{0,7},{9,8},{10,9},{11,1... | collective-permute-start | bytes 147464 | tf_op jit(solution)/shard_map/ppermute | solution.py:26
  59.1 1.9 collective-permute-start.3
  61.1 0.6 fusion.2
  62.1 8.4 %collective-permute-done.3 = f32[3,8,1,256]{3,2,1,0:T(1,128)S(1)} collective-permute-done((f32[3,8,1,256]{3,2,1,0:T(1,128)S(1)}, f32[3,8,1,256]{3,2,1,0:T(1,128)S(1)}, u32[]{:S(2)}, u32[]{:S(2)}) %collective-permute-start.3) | collective-permute-done | bytes 24608 | tf_op jit(solution)/shard_map/ppermute | solution.py:25
  70.6 0.3 fusion.149
  71.0 14.1 %collective-permute-start.9 = (f32[3,1,8,256]{3,2,1,0:T(8,128)S(1)}, f32[3,1,8,256]{3,2,1,0:T(8,128)S(1)}, u32[]{:S(2)}, u32[]{:S(2)}) collective-permute-start(f32[3,1,8,256]{3,2,1,0:T(8,128)S(1)} %get-tuple-element.59), channel_id=1, source_target_pairs={{0,8},{8,16},{16,24},{24,32},{32,40},{40,48},{48,56},{56,64},{64,7... | collective-permute-start | bytes 73736 | tf_op jit(solution)/shard_map/ppermute | solution.py:25
  85.1 6.9 %collective-permute-start.8 = (f32[3,1,8,256]{3,2,1,0:T(8,128)S(1)}, f32[3,1,8,256]{3,2,1,0:T(8,128)S(1)}, u32[]{:S(2)}, u32[]{:S(2)}) collective-permute-start(f32[3,1,8,256]{3,2,1,0:T(8,128)S(1)} %get-tuple-element.60), channel_id=1, source_target_pairs={{8,0},{16,8},{24,16},{32,24},{40,32},{48,40},{56,48},{64,56},{72,6... | collective-permute-start | bytes 73736 | tf_op jit(solution)/shard_map/ppermute | solution.py:26
  92.0 1.9 collective-permute-start.10
  93.9 3.4 %collective-permute-start.11 = (f32[3,8,1,256]{3,2,1,0:T(1,128)S(1)}, f32[3,8,1,256]{3,2,1,0:T(1,128)S(1)}, u32[]{:S(2)}, u32[]{:S(2)}) collective-permute-start(f32[3,8,1,256]{3,2,1,0:T(1,128)S(1)} %get-tuple-element.58), channel_id=1, source_target_pairs={{0,1},{1,2},{2,3},{3,4},{4,5},{5,6},{6,7},{7,0},{8,9},{9,10},{10,1... | collective-permute-start | bytes 73736 | tf_op jit(solution)/shard_map/ppermute | solution.py:25
  97.5 0.6 gather_fusion.1
  98.1 0.9 collective-permute-done.8
  98.9 6.4 %collective-permute-done.11 = f32[3,8,1,256]{3,2,1,0:T(1,128)S(1)} collective-permute-done((f32[3,8,1,256]{3,2,1,0:T(1,128)S(1)}, f32[3,8,1,256]{3,2,1,0:T(1,128)S(1)}, u32[]{:S(2)}, u32[]{:S(2)}) %collective-permute-start.11) | collective-permute-done | bytes 24608 | tf_op jit(solution)/shard_map/ppermute | solution.py:25
  105.6 0.3 fusion.150
  105.9 8.3 %collective-permute-start.13 = (f32[3,1,8,256]{3,2,1,0:T(8,128)S(1)}, f32[3,1,8,256]{3,2,1,0:T(8,128)S(1)}, u32[]{:S(2)}, u32[]{:S(2)}) collective-permute-start(f32[3,1,8,256]{3,2,1,0:T(8,128)S(1)} %get-tuple-element.49), channel_id=1, source_target_pairs={{0,8},{8,16},{16,24},{24,32},{32,40},{40,48},{48,56},{56,64},{64,7... | collective-permute-start | bytes 73736 | tf_op jit(solution)/shard_map/ppermute | solution.py:25
  114.2 11.1 %collective-permute-start.12 = (f32[3,1,8,256]{3,2,1,0:T(8,128)S(1)}, f32[3,1,8,256]{3,2,1,0:T(8,128)S(1)}, u32[]{:S(2)}, u32[]{:S(2)}) collective-permute-start(f32[3,1,8,256]{3,2,1,0:T(8,128)S(1)} %get-tuple-element.50), channel_id=1, source_target_pairs={{8,0},{16,8},{24,16},{32,24},{40,32},{48,40},{56,48},{64,56},{72,6... | collective-permute-start | bytes 73736 | tf_op jit(solution)/shard_map/ppermute | solution.py:26
  125.3 1.9 collective-permute-start.14
  127.2 3.4 %collective-permute-start.15 = (f32[3,8,1,256]{3,2,1,0:T(1,128)S(1)}, f32[3,8,1,256]{3,2,1,0:T(1,128)S(1)}, u32[]{:S(2)}, u32[]{:S(2)}) collective-permute-start(f32[3,8,1,256]{3,2,1,0:T(1,128)S(1)} %get-tuple-element.48), channel_id=1, source_target_pairs={{0,1},{1,2},{2,3},{3,4},{4,5},{5,6},{6,7},{7,0},{8,9},{9,10},{10,1... | collective-permute-start | bytes 73736 | tf_op jit(solution)/shard_map/ppermute | solution.py:25
  130.7 0.6 gather_fusion.3
  131.3 7.4 %collective-permute-done.15 = f32[3,8,1,256]{3,2,1,0:T(1,128)S(1)} collective-permute-done((f32[3,8,1,256]{3,2,1,0:T(1,128)S(1)}, f32[3,8,1,256]{3,2,1,0:T(1,128)S(1)}, u32[]{:S(2)}, u32[]{:S(2)}) %collective-permute-start.15) | collective-permute-done | bytes 24608 | tf_op jit(solution)/shard_map/ppermute | solution.py:25
  138.9 0.3 fusion.151
  139.3 4.1 %collective-permute-start.17 = (f32[3,1,8,256]{3,2,1,0:T(8,128)S(1)}, f32[3,1,8,256]{3,2,1,0:T(8,128)S(1)}, u32[]{:S(2)}, u32[]{:S(2)}) collective-permute-start(f32[3,1,8,256]{3,2,1,0:T(8,128)S(1)} %get-tuple-element.39), channel_id=1, source_target_pairs={{0,8},{8,16},{16,24},{24,32},{32,40},{40,48},{48,56},{56,64},{64,7... | collective-permute-start | bytes 73736 | tf_op jit(solution)/shard_map/ppermute | solution.py:25
  143.4 15.2 %collective-permute-start.16 = (f32[3,1,8,256]{3,2,1,0:T(8,128)S(1)}, f32[3,1,8,256]{3,2,1,0:T(8,128)S(1)}, u32[]{:S(2)}, u32[]{:S(2)}) collective-permute-start(f32[3,1,8,256]{3,2,1,0:T(8,128)S(1)} %get-tuple-element.40), channel_id=1, source_target_pairs={{8,0},{16,8},{24,16},{32,24},{40,32},{48,40},{56,48},{64,56},{72,6... | collective-permute-start | bytes 73736 | tf_op jit(solution)/shard_map/ppermute | solution.py:26
  158.7 1.9 collective-permute-start.18
  160.6 3.4 %collective-permute-start.19 = (f32[3,8,1,256]{3,2,1,0:T(1,128)S(1)}, f32[3,8,1,256]{3,2,1,0:T(1,128)S(1)}, u32[]{:S(2)}, u32[]{:S(2)}) collective-permute-start(f32[3,8,1,256]{3,2,1,0:T(1,128)S(1)} %get-tuple-element.38), channel_id=1, source_target_pairs={{0,1},{1,2},{2,3},{3,4},{4,5},{5,6},{6,7},{7,0},{8,9},{9,10},{10,1... | collective-permute-start | bytes 73736 | tf_op jit(solution)/shard_map/ppermute | solution.py:25
  164.1 0.6 gather_fusion.5
  164.7 7.4 %collective-permute-done.19 = f32[3,8,1,256]{3,2,1,0:T(1,128)S(1)} collective-permute-done((f32[3,8,1,256]{3,2,1,0:T(1,128)S(1)}, f32[3,8,1,256]{3,2,1,0:T(1,128)S(1)}, u32[]{:S(2)}, u32[]{:S(2)}) %collective-permute-start.19) | collective-permute-done | bytes 24608 | tf_op jit(solution)/shard_map/ppermute | solution.py:25
  172.3 0.6 gather_fusion.7
  175.6 6.3 %psum.174 = f32[96]{0:T(128)S(1)} all-reduce(f32[96]{0:T(128)S(1)} %add_add_fusion), channel_id=1, replica_groups=mesh['gx_0'=4,'gx_1'=4,'gx_2'=2,'gx_3'=2,'gy'=8] {'gx_0'}, use_global_device_ids=true, to_apply=%region_2.4 | all-reduce | flops 96 | bytes 768 | tf_op jit(solution)/shard_map/psum | solution.py:38
  181.9 6.0 %psum.171 = f32[96]{0:T(128)S(1)} all-reduce(f32[96]{0:T(128)S(1)} %psum.174), channel_id=1, replica_groups=mesh['gx_0'=4,'gx_1'=4,'gx_2'=2,'gx_3'=2,'gy'=8] {'gx_1'}, use_global_device_ids=true, to_apply=%region_3.5 | all-reduce | flops 96 | bytes 768 | tf_op jit(solution)/shard_map/psum | solution.py:38
  187.9 19.5 %psum.168 = f32[96]{0:T(128)S(1)} all-reduce(f32[96]{0:T(128)S(1)} %psum.171), channel_id=1, replica_groups=mesh['gx_0'=4,'gx_1'=4,'gx_2'=2,'gx_3'=2,'gy'=8] {'gx_2'}, use_global_device_ids=true, to_apply=%region_4.6 | all-reduce | flops 96 | bytes 768 | tf_op jit(solution)/shard_map/psum | solution.py:38
  207.5 14.8 %psum.165 = f32[96]{0:T(128)S(1)} all-reduce(f32[96]{0:T(128)S(1)} %psum.168), channel_id=1, replica_groups=mesh['gx_0'=4,'gx_1'=4,'gx_2'=2,'gx_3'=2,'gy'=8] {'gx_3'}, use_global_device_ids=true, to_apply=%region_5.7 | all-reduce | flops 96 | bytes 768 | tf_op jit(solution)/shard_map/psum | solution.py:38
  222.3 21.6 %psum.162 = f32[96]{0:T(128)S(1)} all-reduce(f32[96]{0:T(128)S(1)} %psum.165), channel_id=1, replica_groups=mesh['gx_0'=4,'gx_1'=4,'gx_2'=2,'gx_3'=2,'gy'=8] {'gy'}, use_global_device_ids=true, to_apply=%region_6.8 | all-reduce | flops 96 | bytes 768 | tf_op jit(solution)/shard_map/psum | solution.py:38
  243.9 0.5 fusion.136
  (97 shorter events, 5.0 us)
Async XLA Ops:
  0.6 172.3 %copy-start = (bf16[1,1,8,64,512]{4,3,2,1,0:T(8,128)(2,1)S(1)}, bf16[1,1,8,64,512]{4,3,2,1,0:T(8,128)(2,1)}, u32[]{:S(2)}) copy-start(bf16[1,1,8,64,512]{4,3,2,1,0:T(8,128)(2,1)} %param.14) | copy-start | bytes 1572868
  0.6 40.5 %copy-start.2 = (bf16[4,3,8,8,256]{4,3,2,1,0:T(8,128)(2,1)S(1)}, bf16[4,3,8,8,256]{4,3,2,1,0:T(8,128)(2,1)}, u32[]{:S(2)}) copy-start(bf16[4,3,8,8,256]{4,3,2,1,0:T(8,128)(2,1)} %param.11) | copy-start | bytes 1179652
  0.7 34.8 %copy-start.7 = (s32[1,1,8]{2,1,0:T(1,128)S(1)}, s32[1,1,8]{2,1,0:T(1,128)}, u32[]{:S(2)}) copy-start(s32[1,1,8]{2,1,0:T(1,128)} %param.16) | copy-start | bytes 100
  0.7 34.9 %copy-start.4 = (s32[4]{0:T(128)S(1)}, s32[4]{0:T(128)}, u32[]{:S(2)}) copy-start(s32[4]{0:T(128)} %param.12) | copy-start | bytes 52
  1.6 47.4 %collective-permute-start.5 = (bf16[4,3,1,8,256]{4,3,2,1,0:T(8,128)(2,1)S(1)}, bf16[4,3,1,8,256]{4,3,2,1,0:T(8,128)(2,1)S(1)}, u32[]{:S(2)}, u32[]{:S(2)}) collective-permute-start(bf16[4,3,1,8,256]{4,3,2,1,0:T(8,128)(2,1)S(1)} %get-tuple-element.29), channel_id=1, source_target_pairs={{8,0},{16,8},{24,16},{32,24},{40,32},{48,40},{56,48},{64,56},{72,6... | collective-permute-start | bytes 147464 | tf_op jit(solution)/shard_map/ppermute | solution.py:26
  10.3 36.7 %collective-permute-start.4 = (bf16[4,3,1,8,256]{4,3,2,1,0:T(8,128)(2,1)S(1)}, bf16[4,3,1,8,256]{4,3,2,1,0:T(8,128)(2,1)S(1)}, u32[]{:S(2)}, u32[]{:S(2)}) collective-permute-start(bf16[4,3,1,8,256]{4,3,2,1,0:T(8,128)(2,1)S(1)} %get-tuple-element.30), channel_id=1, source_target_pairs={{0,8},{8,16},{16,24},{24,32},{32,40},{40,48},{48,56},{56,64},{64,7... | collective-permute-start | bytes 147464 | tf_op jit(solution)/shard_map/ppermute | solution.py:25
  21.7 40.3 %collective-permute-start.1 = (f32[3,1,8,256]{3,2,1,0:T(8,128)S(1)}, f32[3,1,8,256]{3,2,1,0:T(8,128)S(1)}, u32[]{:S(2)}, u32[]{:S(2)}) collective-permute-start(f32[3,1,8,256]{3,2,1,0:T(8,128)S(1)} %get-tuple-element.69), channel_id=1, source_target_pairs={{0,8},{8,16},{16,24},{24,32},{32,40},{40,48},{48,56},{56,64},{64,7... | collective-permute-start | bytes 73736 | tf_op jit(solution)/shard_map/ppermute | solution.py:25
  24.1 37.9 %collective-permute-start = (f32[3,1,8,256]{3,2,1,0:T(8,128)S(1)}, f32[3,1,8,256]{3,2,1,0:T(8,128)S(1)}, u32[]{:S(2)}, u32[]{:S(2)}) collective-permute-start(f32[3,1,8,256]{3,2,1,0:T(8,128)S(1)} %get-tuple-element.70), channel_id=1, source_target_pairs={{8,0},{16,8},{24,16},{32,24},{40,32},{48,40},{56,48},{64,56},{72,6... | collective-permute-start | bytes 73736 | tf_op jit(solution)/shard_map/ppermute | solution.py:26
  30.1 32.0 %collective-permute-start.2 = (f32[3,8,1,256]{3,2,1,0:T(1,128)S(1)}, f32[3,8,1,256]{3,2,1,0:T(1,128)S(1)}, u32[]{:S(2)}, u32[]{:S(2)}) collective-permute-start(f32[3,8,1,256]{3,2,1,0:T(1,128)S(1)} %get-tuple-element.67), channel_id=1, source_target_pairs={{1,0},{2,1},{3,2},{4,3},{5,4},{6,5},{7,6},{0,7},{9,8},{10,9},{11,1... | collective-permute-start | bytes 73736 | tf_op jit(solution)/shard_map/ppermute | solution.py:26
  47.0 12.1 %collective-permute-start.6 = (bf16[4,3,8,1,256]{4,3,2,1,0:T(2,128)(2,1)S(1)}, bf16[4,3,8,1,256]{4,3,2,1,0:T(2,128)(2,1)S(1)}, u32[]{:S(2)}, u32[]{:S(2)}) collective-permute-start(bf16[4,3,8,1,256]{4,3,2,1,0:T(2,128)(2,1)S(1)} %get-tuple-element.27), channel_id=1, source_target_pairs={{0,1},{1,2},{2,3},{3,4},{4,5},{5,6},{6,7},{7,0},{8,9},{9,10},{10,1... | collective-permute-start | bytes 147464 | tf_op jit(solution)/shard_map/ppermute | solution.py:25
  49.0 12.0 %collective-permute-start.7 = (bf16[4,3,8,1,256]{4,3,2,1,0:T(2,128)(2,1)S(1)}, bf16[4,3,8,1,256]{4,3,2,1,0:T(2,128)(2,1)S(1)}, u32[]{:S(2)}, u32[]{:S(2)}) collective-permute-start(bf16[4,3,8,1,256]{4,3,2,1,0:T(2,128)(2,1)S(1)} %get-tuple-element.28), channel_id=1, source_target_pairs={{1,0},{2,1},{3,2},{4,3},{5,4},{6,5},{7,6},{0,7},{9,8},{10,9},{11,1... | collective-permute-start | bytes 147464 | tf_op jit(solution)/shard_map/ppermute | solution.py:26
  59.1 11.3 %collective-permute-start.3 = (f32[3,8,1,256]{3,2,1,0:T(1,128)S(1)}, f32[3,8,1,256]{3,2,1,0:T(1,128)S(1)}, u32[]{:S(2)}, u32[]{:S(2)}) collective-permute-start(f32[3,8,1,256]{3,2,1,0:T(1,128)S(1)} %get-tuple-element.68), channel_id=1, source_target_pairs={{0,1},{1,2},{2,3},{3,4},{4,5},{5,6},{6,7},{7,0},{8,9},{9,10},{10,1... | collective-permute-start | bytes 73736 | tf_op jit(solution)/shard_map/ppermute | solution.py:25
  62.0 8.7 %copy-start.1 = (f32[256,256]{1,0:T(8,128)S(1)}, f32[256,256]{1,0:T(8,128)}, u32[]{:S(2)}) copy-start(f32[256,256]{1,0:T(8,128)} %param.13) | copy-start | bytes 786436
  71.0 27.0 %collective-permute-start.9 = (f32[3,1,8,256]{3,2,1,0:T(8,128)S(1)}, f32[3,1,8,256]{3,2,1,0:T(8,128)S(1)}, u32[]{:S(2)}, u32[]{:S(2)}) collective-permute-start(f32[3,1,8,256]{3,2,1,0:T(8,128)S(1)} %get-tuple-element.59), channel_id=1, source_target_pairs={{0,8},{8,16},{16,24},{24,32},{32,40},{40,48},{48,56},{56,64},{64,7... | collective-permute-start | bytes 73736 | tf_op jit(solution)/shard_map/ppermute | solution.py:25
  85.1 13.9 %collective-permute-start.8 = (f32[3,1,8,256]{3,2,1,0:T(8,128)S(1)}, f32[3,1,8,256]{3,2,1,0:T(8,128)S(1)}, u32[]{:S(2)}, u32[]{:S(2)}) collective-permute-start(f32[3,1,8,256]{3,2,1,0:T(8,128)S(1)} %get-tuple-element.60), channel_id=1, source_target_pairs={{8,0},{16,8},{24,16},{32,24},{40,32},{48,40},{56,48},{64,56},{72,6... | collective-permute-start | bytes 73736 | tf_op jit(solution)/shard_map/ppermute | solution.py:26
  92.0 7.0 %collective-permute-start.10 = (f32[3,8,1,256]{3,2,1,0:T(1,128)S(1)}, f32[3,8,1,256]{3,2,1,0:T(1,128)S(1)}, u32[]{:S(2)}, u32[]{:S(2)}) collective-permute-start(f32[3,8,1,256]{3,2,1,0:T(1,128)S(1)} %get-tuple-element.57), channel_id=1, source_target_pairs={{1,0},{2,1},{3,2},{4,3},{5,4},{6,5},{7,6},{0,7},{9,8},{10,9},{11,1... | collective-permute-start | bytes 73736 | tf_op jit(solution)/shard_map/ppermute | solution.py:26
  93.9 11.5 %collective-permute-start.11 = (f32[3,8,1,256]{3,2,1,0:T(1,128)S(1)}, f32[3,8,1,256]{3,2,1,0:T(1,128)S(1)}, u32[]{:S(2)}, u32[]{:S(2)}) collective-permute-start(f32[3,8,1,256]{3,2,1,0:T(1,128)S(1)} %get-tuple-element.58), channel_id=1, source_target_pairs={{0,1},{1,2},{2,3},{3,4},{4,5},{5,6},{6,7},{7,0},{8,9},{9,10},{10,1... | collective-permute-start | bytes 73736 | tf_op jit(solution)/shard_map/ppermute | solution.py:25
  105.9 25.3 %collective-permute-start.13 = (f32[3,1,8,256]{3,2,1,0:T(8,128)S(1)}, f32[3,1,8,256]{3,2,1,0:T(8,128)S(1)}, u32[]{:S(2)}, u32[]{:S(2)}) collective-permute-start(f32[3,1,8,256]{3,2,1,0:T(8,128)S(1)} %get-tuple-element.49), channel_id=1, source_target_pairs={{0,8},{8,16},{16,24},{24,32},{32,40},{40,48},{48,56},{56,64},{64,7... | collective-permute-start | bytes 73736 | tf_op jit(solution)/shard_map/ppermute | solution.py:25
  114.2 17.1 %collective-permute-start.12 = (f32[3,1,8,256]{3,2,1,0:T(8,128)S(1)}, f32[3,1,8,256]{3,2,1,0:T(8,128)S(1)}, u32[]{:S(2)}, u32[]{:S(2)}) collective-permute-start(f32[3,1,8,256]{3,2,1,0:T(8,128)S(1)} %get-tuple-element.50), channel_id=1, source_target_pairs={{8,0},{16,8},{24,16},{32,24},{40,32},{48,40},{56,48},{64,56},{72,6... | collective-permute-start | bytes 73736 | tf_op jit(solution)/shard_map/ppermute | solution.py:26
  125.3 6.0 %collective-permute-start.14 = (f32[3,8,1,256]{3,2,1,0:T(1,128)S(1)}, f32[3,8,1,256]{3,2,1,0:T(1,128)S(1)}, u32[]{:S(2)}, u32[]{:S(2)}) collective-permute-start(f32[3,8,1,256]{3,2,1,0:T(1,128)S(1)} %get-tuple-element.47), channel_id=1, source_target_pairs={{1,0},{2,1},{3,2},{4,3},{5,4},{6,5},{7,6},{0,7},{9,8},{10,9},{11,1... | collective-permute-start | bytes 73736 | tf_op jit(solution)/shard_map/ppermute | solution.py:26
  127.2 11.5 %collective-permute-start.15 = (f32[3,8,1,256]{3,2,1,0:T(1,128)S(1)}, f32[3,8,1,256]{3,2,1,0:T(1,128)S(1)}, u32[]{:S(2)}, u32[]{:S(2)}) collective-permute-start(f32[3,8,1,256]{3,2,1,0:T(1,128)S(1)} %get-tuple-element.48), channel_id=1, source_target_pairs={{0,1},{1,2},{2,3},{3,4},{4,5},{5,6},{6,7},{7,0},{8,9},{9,10},{10,1... | collective-permute-start | bytes 73736 | tf_op jit(solution)/shard_map/ppermute | solution.py:25
  139.3 25.4 %collective-permute-start.17 = (f32[3,1,8,256]{3,2,1,0:T(8,128)S(1)}, f32[3,1,8,256]{3,2,1,0:T(8,128)S(1)}, u32[]{:S(2)}, u32[]{:S(2)}) collective-permute-start(f32[3,1,8,256]{3,2,1,0:T(8,128)S(1)} %get-tuple-element.39), channel_id=1, source_target_pairs={{0,8},{8,16},{16,24},{24,32},{32,40},{40,48},{48,56},{56,64},{64,7... | collective-permute-start | bytes 73736 | tf_op jit(solution)/shard_map/ppermute | solution.py:25
  143.4 21.2 %collective-permute-start.16 = (f32[3,1,8,256]{3,2,1,0:T(8,128)S(1)}, f32[3,1,8,256]{3,2,1,0:T(8,128)S(1)}, u32[]{:S(2)}, u32[]{:S(2)}) collective-permute-start(f32[3,1,8,256]{3,2,1,0:T(8,128)S(1)} %get-tuple-element.40), channel_id=1, source_target_pairs={{8,0},{16,8},{24,16},{32,24},{40,32},{48,40},{56,48},{64,56},{72,6... | collective-permute-start | bytes 73736 | tf_op jit(solution)/shard_map/ppermute | solution.py:26
  158.7 6.0 %collective-permute-start.18 = (f32[3,8,1,256]{3,2,1,0:T(1,128)S(1)}, f32[3,8,1,256]{3,2,1,0:T(1,128)S(1)}, u32[]{:S(2)}, u32[]{:S(2)}) collective-permute-start(f32[3,8,1,256]{3,2,1,0:T(1,128)S(1)} %get-tuple-element.37), channel_id=1, source_target_pairs={{1,0},{2,1},{3,2},{4,3},{5,4},{6,5},{7,6},{0,7},{9,8},{10,9},{11,1... | collective-permute-start | bytes 73736 | tf_op jit(solution)/shard_map/ppermute | solution.py:26
  160.6 11.5 %collective-permute-start.19 = (f32[3,8,1,256]{3,2,1,0:T(1,128)S(1)}, f32[3,8,1,256]{3,2,1,0:T(1,128)S(1)}, u32[]{:S(2)}, u32[]{:S(2)}) collective-permute-start(f32[3,8,1,256]{3,2,1,0:T(1,128)S(1)} %get-tuple-element.38), channel_id=1, source_target_pairs={{0,1},{1,2},{2,3},{3,4},{4,5},{5,6},{6,7},{7,0},{8,9},{9,10},{10,1... | collective-permute-start | bytes 73736 | tf_op jit(solution)/shard_map/ppermute | solution.py:25
  172.3 1.6 copy-start.3
  174.5 1.0 copy-start.5
  174.5 69.4 %copy-start.6 = (s32[96]{0:T(128)S(1)}, s32[96]{0:T(128)}, u32[]{:S(2)}) copy-start(s32[96]{0:T(128)} %param.17) | copy-start | bytes 1156
where the time goes:
time: 249 us; the launch traced here: 244 us
  starting transfers between devices  122 us (49%)
  blocking collectives  68.3 us (27%)
  waiting for transfers between devices  30.5 us (12%)
  between operations  8.93 us (4%)
  local copies, waits for them, and re-layouts  6.62 us (3%)
  matrix products  4.31 us (2%)
  other arithmetic  4.05 us (2%)
    ppermute x10, starting transfers between devices, padded_2(): lax.ppermute(initial, axis, [(b, a) for a, b in up])  68.9 us
    psum x5, blocking collectives, over_axes(): return functools.reduce(lax.psum, axes, x)  68.3 us
    ppermute x10, starting transfers between devices, padded_2(): lax.ppermute(last, axis, up)  52.8 us
    ppermute x10, waiting for transfers between devices, padded_2(): lax.ppermute(last, axis, up)  29.6 us
  transfers between devices with their start and end apart: 20, of which 5 were waited for; matrix products, arithmetic and copies ran while one was open for 3% of the time, Pallas kernels for 0%

commit v1 on v0

v1 whole, which is shorter than its diff:
```python
import functools

import jax
import jax.numpy as jnp
from jax import lax
from jax.experimental import pallas as pl
from jax.experimental.pallas import tpu as pltpu
from jax.sharding import Mesh
from jax.sharding import PartitionSpec as P

STEPS = 4
GX = ("gx_0", "gx_1", "gx_2", "gx_3")
NEAR_AXES = ("gx_0", "gx_1", "gx_3")
FAR_AXES = ("gx_2", "gy")
TENTH = 0.2 * 0.5
RADII = (4, 4, 3, 2, 1, 2)
REST = 5
LEVELS = 256


def x_base(field):
    return 3 * sum(RADII[:field])


def x_tile(field, c, d):
    return x_base(field) + c * RADII[field] + d - 1


X_TILES = x_base(len(RADII))


def y_pairs(field):
    return 3 + RADII[field]


def y_tile(field, c, i):
    return 3 * sum(y_pairs(f) for f in range(field)) + c * y_pairs(field) + i


Y_TILES = y_tile(len(RADII) - 1, 2, y_pairs(len(RADII) - 1) - 1) + 1


def own_column(adj_ref, st_ref, place, field, c, x):
    if field == 0:
        return adj_ref[c, x]
    if field == REST:
        return adj_ref[c, x] - adj_ref[c, x].astype(jnp.bfloat16).astype(jnp.float32)
    return st_ref[place[field - 1], c, x]


def pack_x(place, adj_ref, st_ref, far_ref, near_ref):
    first = place[4] == 0
    for field, radius in enumerate(RADII):
        for d in range(1, radius + 1):
            far_x = jnp.where(first, d - 1, 8 - d)
            near_x = jnp.where(first, 8 - d, d - 1)
            for c in range(3):
                n = x_tile(field, c, d)
                far_ref[n] = own_column(adj_ref, st_ref, place, field, c, far_x).astype(jnp.bfloat16)
                near_ref[n] = own_column(adj_ref, st_ref, place, field, c, near_x).astype(jnp.bfloat16)


def column(place, adj_ref, st_ref, far_ref, near_ref, field, c, x):
    if 0 <= x < 8:
        return own_column(adj_ref, st_ref, place, field, c, x).astype(jnp.float32)
    n = x_tile(field, c, -x if x < 0 else x - 7)
    far, near = far_ref[n].astype(jnp.float32), near_ref[n].astype(jnp.float32)
    return jnp.where((place[4] == 0) == (x < 0), far, near)


def low_half():
    return lax.broadcasted_iota(jnp.int32, (8, LEVELS), 0) < 4


def swap_halves(tile):
    return pltpu.roll(tile, 4, 0)


def pack_y(place, adj_ref, st_ref, far_ref, near_ref, even_ref, odd_ref):
    even = place[5] == 0
    low = low_half()
    for field, radius in enumerate(RADII):
        for c in range(3):
            for i in range(y_pairs(field)):
                x = 2 * i - (radius - 1)
                left = column(place, adj_ref, st_ref, far_ref, near_ref, field, c, x)
                right = column(place, adj_ref, st_ref, far_ref, near_ref, field, c, x + 1)
                bottom = jnp.where(low, left, swap_halves(right))
                top = jnp.where(low, swap_halves(left), right)
                n = y_tile(field, c, i)
                even_ref[n] = jnp.where(even, top, bottom).astype(jnp.bfloat16)
                odd_ref[n] = jnp.where(even, bottom, top).astype(jnp.bfloat16)


def sweep(
    place,
    tiles,
    turbines,
    adj_ref,
    st_ref,
    far_ref,
    near_ref,
    even_ref,
    odd_ref,
    whi_ref,
    wlo_ref,
    dz_ref,
    filt_ref,
    out_ref,
    part_ref,
    ext,
    solved,
    state_dz,
    kept,
    picked,
):
    even = place[5] == 0
    low = low_half()
    for field, radius in enumerate(RADII):
        into = 0 if field == REST else field
        for c in range(3):
            for x in range(-radius, 8 + radius):
                if field == REST and 0 <= x < 8:
                    continue
                tile = column(place, adj_ref, st_ref, far_ref, near_ref, field, c, x)
                if field == REST:
                    tile += ext[0, c, x + 4, 0:8, :]
                ext[into, c, x + 4, 0:8, :] = tile
            for i in range(y_pairs(field)):
                x = 2 * i - (radius - 1)
                n = y_tile(field, c, i)
                a, b = even_ref[n].astype(jnp.float32), odd_ref[n].astype(jnp.float32)
                plus, minus = jnp.where(even, a, b), jnp.where(even, b, a)
                left = jnp.where(low, plus, swap_halves(minus))
                right = jnp.where(low, swap_halves(plus), minus)
                if field == REST:
                    left += ext[0, c, x + 4, 8:16, :]
                    right += ext[0, c, x + 5, 8:16, :]
                ext[into, c, x + 4, 8:16, :] = left
                ext[into, c, x + 5, 8:16, :] = right

    for step in range(STEPS):
        reach = 3 - step
        lo, hi = 4 - reach, 12 + reach
        wide = hi - lo + 2
        rows = ext[0, :, lo - 1 : hi + 1].reshape(3 * wide * 16, LEVELS)
        upper = rows.astype(jnp.bfloat16)
        lower = (rows - upper.astype(jnp.float32)).astype(jnp.bfloat16)
        for half in range(2):
            lanes = slice(half * LEVELS, (half + 1) * LEVELS)
            total = jnp.dot(upper, whi_ref[:, lanes], preferred_element_type=jnp.float32)
            total += jnp.dot(lower, whi_ref[:, lanes], preferred_element_type=jnp.float32)
            total += jnp.dot(upper, wlo_ref[:, lanes], preferred_element_type=jnp.float32)
            solved[half, :, lo - 1 : hi + 1] = total.reshape(3, wide, 16, LEVELS)
        field = 1 + step
        states = ext[field, :, lo:hi].reshape(3 * (wide - 2) * 16, LEVELS).astype(jnp.bfloat16)
        state_dz[:, lo:hi] = jnp.dot(
            states, dz_ref[...], preferred_element_type=jnp.float32
        ).reshape(3, wide - 2, 16, LEVELS)

        def one(e, carry):
            def across(ref, *at):
                return ref[(*at, e + 1)] - ref[(*at, e - 1)]

            def along(tile):
                return pltpu.roll(tile, 15, 0) - pltpu.roll(tile, 1, 0)

            sol = [solved[0, c, e] for c in range(3)]
            vel = [ext[field, c, e] for c in range(3)]
            derivs = (
                [across(ext, field, c) for c in range(3)],
                [along(vel[c]) for c in range(3)],
                [state_dz[c, e] for c in range(3)],
            )
            for c in range(3):
                advect = vel[0] * across(solved, 0, c) + vel[1] * along(sol[c]) + vel[2] * solved[1, c, e]
                couple = sol[0] * derivs[c][0] + sol[1] * derivs[c][1] + sol[2] * derivs[c][2]
                ext[0, c, e] = sol[c] + TENTH * (advect - couple)
            return carry

        lax.fori_loop(lo, hi, one, 0)
        kept[step] = ext[0, 0, 4:12, 0:8, :]

    out_ref[...] = ext[0, :, 4:12, 0:8, :]
    lane = lax.broadcasted_iota(jnp.int32, (1, 128), 1)
    total = jnp.zeros((1, 128), jnp.float32)
    for slot in range(8):
        tile = tiles[slot]
        x, y = tile // 4, 2 * lax.rem(tile, 4)
        for step in range(STEPS):
            for k in range(2):
                lanes = slice(k * LEVELS, (k + 1) * LEVELS)
                picked[slot, step : step + 1, lanes] = kept[step, x, pl.ds(y + k, 1), :]
                picked[slot, 4 + step : 5 + step, lanes] = ext[1 + step, 0, x + 4, pl.ds(y + k, 1), :]
        both = lax.dot_general(
            picked[slot].astype(jnp.bfloat16),
            filt_ref[slot],
            (((1,), (1,)), ((), ())),
            preferred_element_type=jnp.float32,
        )
        sampled, speeds = both[0:4], both[4:8]
        term = jnp.sum(jnp.sum(speeds * speeds * sampled, axis=1, keepdims=True), axis=0, keepdims=True)
        total += jnp.where(lane == turbines[slot], term * (1.0 / 64.0), 0.0)
    part_ref[...] = jnp.broadcast_to(total, part_ref.shape)


SMEM = pl.BlockSpec(memory_space=pltpu.SMEM)
VMEM = pl.BlockSpec(memory_space=pltpu.VMEM)


def body(
    adjoint_init,
    saved_states,
    step_index,
    vertical_inverse,
    disk_filter,
    pair_turbine,
    pair_tile,
    turbine_owner,
):
    turbines = turbine_owner.shape[0]
    place = jnp.concatenate(
        [
            step_index.astype(jnp.int32),
            lax.axis_index("gx_3").astype(jnp.int32)[None],
            lax.rem(lax.axis_index("gy"), 2).astype(jnp.int32)[None],
        ]
    )
    blocks, slabs = lax.axis_size(GX), lax.axis_size("gy")
    near = [(i, i ^ 1) for i in range(blocks)]
    far = [(i, (i + 1) % blocks if i % 2 else (i - 1) % blocks) for i in range(blocks)]
    evens = [(i, i ^ 1) for i in range(slabs)]
    odds = [(i, (i + 1) % slabs if i % 2 else (i - 1) % slabs) for i in range(slabs)]

    x_shape = jax.ShapeDtypeStruct((X_TILES, 8, LEVELS), jnp.bfloat16)
    y_shape = jax.ShapeDtypeStruct((Y_TILES, 8, LEVELS), jnp.bfloat16)
    to_far, to_near = pl.pallas_call(
        pack_x,
        out_shape=(x_shape, x_shape),
        in_specs=[SMEM, VMEM, VMEM],
        out_specs=(VMEM, VMEM),
        name="pack_x",
    )(place, adjoint_init, saved_states)
    far_halo = lax.ppermute(to_far, GX, far)
    near_halo = lax.ppermute(to_near, GX, near)

    inverse_dz = jnp.pad(vertical_inverse[:, 1:], ((0, 0), (0, 1))) - jnp.pad(
        vertical_inverse[:, :-1], ((0, 0), (1, 0))
    )
    weights = jnp.concatenate([vertical_inverse, inverse_dz], axis=1)
    upper = lax.reduce_precision(weights, 8, 7)
    whi, wlo = upper.astype(jnp.bfloat16), (weights - upper).astype(jnp.bfloat16)
    k = lax.broadcasted_iota(jnp.int32, (LEVELS, LEVELS), 0)
    z = lax.broadcasted_iota(jnp.int32, (LEVELS, LEVELS), 1)
    dz = ((k == z + 1).astype(jnp.float32) - (k == z - 1).astype(jnp.float32)).astype(jnp.bfloat16)

    to_even, to_odd = pl.pallas_call(
        pack_y,
        out_shape=(y_shape, y_shape),
        in_specs=[SMEM] + [VMEM] * 4,
        out_specs=(VMEM, VMEM),
        name="pack_y",
    )(place, adjoint_init, saved_states, far_halo, near_halo)
    odd_halo = lax.ppermute(to_odd, "gy", odds)
    even_halo = lax.ppermute(to_even, "gy", evens)

    close = lax.axis_size(NEAR_AXES)
    wide = lax.axis_size(FAR_AXES)
    adjoint, part = pl.pallas_call(
        sweep,
        out_shape=(
            jax.ShapeDtypeStruct(adjoint_init.shape, jnp.float32),
            jax.ShapeDtypeStruct((close, 128), jnp.float32),
        ),
        in_specs=[SMEM] * 3 + [VMEM] * 10,
        out_specs=(VMEM, VMEM),
        scratch_shapes=[
            pltpu.VMEM((5, 3, 16, 16, LEVELS), jnp.float32),
            pltpu.VMEM((2, 3, 16, 16, LEVELS), jnp.float32),
            pltpu.VMEM((3, 16, 16, LEVELS), jnp.float32),
            pltpu.VMEM((STEPS, 8, 8, LEVELS), jnp.float32),
            pltpu.VMEM((8, 8, 2 * LEVELS), jnp.float32),
        ],
        name="sweep",
    )(
        place,
        pair_tile[0, 0],
        pair_turbine[0, 0],
        adjoint_init,
        saved_states,
        far_halo,
        near_halo,
        even_halo,
        odd_halo,
        whi,
        wlo,
        dz,
        disk_filter[0, 0],
    )
    part = jnp.sum(lax.all_to_all(part, NEAR_AXES, 0, 0, tiled=True), axis=0)
    part = jnp.broadcast_to(part[None], (wide, 128))
    totals = jnp.sum(lax.all_to_all(part, FAR_AXES, 0, 0, tiled=True), axis=0)[:turbines]
    own_index = lax.axis_index(GX) * lax.axis_size("gy") + lax.axis_index("gy")
    turbine_grad = jnp.where(turbine_owner == own_index, totals, jnp.float32(0.0))[None, None, :]
    return (adjoint, turbine_grad)


def solution(mesh):
    torus = Mesh(
        mesh.devices.reshape(4, 4, 2, 2, mesh.shape["gy"]), ("gx_0", "gx_1", "gx_2", "gx_3", "gy")
    )
    placed = (
        P(None, GX, "gy", None),
        P(None, None, GX, "gy", None),
        P(),
        P(),
        P(GX, "gy", None, None, None),
        P(GX, "gy", None),
        P(GX, "gy", None),
        P(),
    )
    return jax.shard_map(
        body,
        mesh=torus,
        in_specs=placed,
        out_specs=(P(None, GX, "gy", None), P(GX, "gy", None)),
        check_vma=False,
    )
```

time: 249 us -> 117 us (0.47); the launches traced: 244 us -> 116 us
  starting transfers between devices: 122 us -> 53.9 us
  blocking collectives: 68.3 us -> 20.2 us
  Pallas kernels: 0 us -> 12.7 us
  between operations: 8.93 us -> 0.76 us
  waiting for transfers between devices: 30.5 us -> 22.4 us
  matrix products: 4.31 us -> 0 us
  local copies, waits for them, and re-layouts: 6.62 us -> 3.45 us
    ppermute x20 -> x4, starting transfers between devices: 122 us -> 44.8 us  [the longest x1 16.8 us: body(): far_halo = lax.ppermute(to_far, GX, far)]
    psum x5 -> x0, blocking collectives: 68.3 us -> none  [over_axes(): return functools.reduce(lax.psum, axes, x)]
    all_to_all x0 -> x1, blocking collectives: none -> 20.2 us  [body(): part = jnp.sum(lax.all_to_all(part, NEAR_AXES, 0, 0, tiled=True), axis=0)]
    ppermute x20 -> x4, waiting for transfers between devices: 30.5 us -> 11.2 us  [the longest x1 10.2 us: body(): odd_halo = lax.ppermute(to_odd, 'gy', odds)]
    pallas_call x0 -> x3, Pallas kernels: none -> 12.7 us  [the longest x1 8.39 us: body(): pl.pallas_call(sweep, out_shape=(jax.ShapeDtypeStruct(adjoint_init.shape,...]
    all_to_all x0 -> x1, waiting for transfers between devices: none -> 11.2 us  [body(): lax.all_to_all(part, FAR_AXES, 0, 0, tiled=True)]
    all_to_all x0 -> x1, starting transfers between devices: none -> 9.13 us  [body(): lax.all_to_all(part, FAR_AXES, 0, 0, tiled=True)]
    gather x8 -> x0, local copies, waits for them, and re-layouts: 4.57 us -> none  [the longest x4 2.28 us: body(): picked_speed = jnp.take(speed_tiles, slot_tiles, axis=0)]
  transfers between devices with their start and end apart: 20 -> 5, of which waited for: 5 -> 3; matrix products, arithmetic and copies ran while one was open for 3% -> 2% of each run, Pallas kernels for 0% -> 0%
where the time goes in v1:
time: 117 us; the launch traced here: 116 us
  starting transfers between devices  53.9 us (46%)
  waiting for transfers between devices  22.4 us (19%)
  blocking collectives  20.2 us (17%)
  Pallas kernels  12.7 us (11%)
  local copies, waits for them, and re-layouts  3.45 us (3%)
  other arithmetic  2.93 us (3%)
    all_to_all x1, blocking collectives, body(): part = jnp.sum(lax.all_to_all(part, NEAR_AXES, 0, 0, tiled=True), axis=0)  20.2 us
    ppermute x1, starting transfers between devices, body(): far_halo = lax.ppermute(to_far, GX, far)  16.8 us
    all_to_all x1, waiting for transfers between devices, body(): lax.all_to_all(part, FAR_AXES, 0, 0, tiled=True)  11.2 us
    ppermute x1, starting transfers between devices, body(): even_halo = lax.ppermute(to_even, 'gy', evens)  11 us
    ppermute x1, starting transfers between devices, body(): odd_halo = lax.ppermute(to_odd, 'gy', odds)  10.6 us
    ppermute x1, waiting for transfers between devices, body(): odd_halo = lax.ppermute(to_odd, 'gy', odds)  10.2 us
    all_to_all x1, starting transfers between devices, body(): lax.all_to_all(part, FAR_AXES, 0, 0, tiled=True)  9.13 us
    pallas_call x1, Pallas kernels, body(): pl.pallas_call(sweep, out_shape=(jax.ShapeDtypeStruct(adjoint_init.shape,...  8.39 us
  transfers between devices with their start and end apart: 5, of which 3 were waited for; matrix products, arithmetic and copies ran while one was open for 2% of the time, Pallas kernels for 0%

profile of v1, /device:TPU:1, one launch (start us, length us, event | category | flops | bytes accessed | tf_op | source)
XLA Modules:
  0.0 116.4 jit_solution(1908078810242235304)
XLA Ops:
  0.6 0.0 copy-start.5
  0.6 0.6 copy-done.5
  1.3 0.6 pad_add_fusion.place
  1.9 0.0 copy-start
  1.9 1.9 %pack_x.1 = (bf16[48,8,256]{2,1,0:T(8,128)(2,1)}, bf16[48,8,256]{2,1,0:T(8,128)(2,1)}) custom-call(s32[6]{0:T(128)} %pad_add_fusion.place, f32[3,8,8,256]{3,2,1,0:T(8,128)} %adj_ref.5, bf16[4,3,8,8,256]{4,3,2,1,0:T(8,128)(2,1)} %st_ref.5), custom_call_target="tpu_custom_call" | custom-call | tf_op jit(solution)/shard_map/pack_x/pallas_call | solution.py:237
  3.9 16.8 %collective-permute-start = (bf16[48,8,256]{2,1,0:T(8,128)(2,1)}, bf16[48,8,256]{2,1,0:T(8,128)(2,1)S(1)}, u32[]{:S(2)}, u32[]{:S(2)}) collective-permute-start(bf16[48,8,256]{2,1,0:T(8,128)(2,1)} %get-tuple-element.8), channel_id=1, source_target_pairs={{0,504},{8,16},{16,8},{24,32},{32,24},{40,48},{48,40},{56,64},{64,... | collective-permute-start | bytes 589832 | tf_op jit(solution)/shard_map/ppermute | solution.py:244
  20.7 6.4 %collective-permute-start.1 = (bf16[48,8,256]{2,1,0:T(8,128)(2,1)}, bf16[48,8,256]{2,1,0:T(8,128)(2,1)S(1)}, u32[]{:S(2)}, u32[]{:S(2)}) collective-permute-start(bf16[48,8,256]{2,1,0:T(8,128)(2,1)} %get-tuple-element.9), channel_id=1, source_target_pairs={{0,8},{8,0},{16,24},{24,16},{32,40},{40,32},{48,56},{56,48},{64,72... | collective-permute-start | bytes 589832 | tf_op jit(solution)/shard_map/ppermute | solution.py:245
  27.1 0.0 copy-done
  27.1 0.1 fusion.2
  27.2 0.1 pad_subtract_fusion
  27.4 0.0 collective-permute-done.far_ref
  27.4 0.0 copy-start.1
  27.4 0.9 collective-permute-done.1.near_ref
  28.3 0.0 copy-done.1
  28.4 0.0 copy-start.2
  28.4 0.7 copy-done.2
  29.0 2.4 %pack_y.1 = (bf16[102,8,256]{2,1,0:T(8,128)(2,1)}, bf16[102,8,256]{2,1,0:T(8,128)(2,1)}) custom-call(s32[6]{0:T(128)} %pad_add_fusion.place, f32[3,8,8,256]{3,2,1,0:T(8,128)} %adj_ref.5, bf16[4,3,8,8,256]{4,3,2,1,0:T(8,128)(2,1)} %st_ref.5, bf16[48,8,256]{2,1,0:T(8,128)(2,1)} %copy-done.1, bf16[48,8,256]{2,1,0:T(8,128)(2,1)} %copy-done.2), custom_call_target="tpu_custom_call" | custom-call | tf_op jit(solution)/shard_map/pack_y/pallas_call | solution.py:257
  31.4 11.0 %collective-permute-start.2 = (bf16[102,8,256]{2,1,0:T(8,128)(2,1)}, bf16[102,8,256]{2,1,0:T(8,128)(2,1)S(1)}, u32[]{:S(2)}, u32[]{:S(2)}) collective-permute-start(bf16[102,8,256]{2,1,0:T(8,128)(2,1)} %get-tuple-element.10), channel_id=1, source_target_pairs={{0,1},{1,0},{2,3},{3,2},{4,5},{5,4},{6,7},{7,6},{8,9},{9,8},{10,11... | collective-permute-start | bytes 1253384 | tf_op jit(solution)/shard_map/ppermute | solution.py:265
  42.4 10.6 %collective-permute-start.3 = (bf16[102,8,256]{2,1,0:T(8,128)(2,1)}, bf16[102,8,256]{2,1,0:T(8,128)(2,1)S(1)}, u32[]{:S(2)}, u32[]{:S(2)}) collective-permute-start(bf16[102,8,256]{2,1,0:T(8,128)(2,1)} %get-tuple-element.11), channel_id=1, source_target_pairs={{0,7},{1,2},{2,1},{3,4},{4,3},{5,6},{6,5},{7,0},{8,15},{9,10},{10,... | collective-permute-start | bytes 1253384 | tf_op jit(solution)/shard_map/ppermute | solution.py:264
  53.0 0.9 fusion
  53.9 0.7 subtract_convert_fusion.dz_ref
  54.6 0.0 collective-permute-done.2.even_ref
  54.6 0.0 copy-start.3
  54.6 10.2 %collective-permute-done.3.odd_ref = bf16[102,8,256]{2,1,0:T(8,128)(2,1)S(1)} collective-permute-done((bf16[102,8,256]{2,1,0:T(8,128)(2,1)}, bf16[102,8,256]{2,1,0:T(8,128)(2,1)S(1)}, u32[]{:S(2)}, u32[]{:S(2)}) %collective-permute-start.3) | collective-permute-done | bytes 417824 | tf_op jit(solution)/shard_map/ppermute | solution.py:264
  64.8 0.0 copy-start.4
  64.8 0.0 copy-done.3
  64.8 0.8 copy-done.4
  65.5 8.4 %sweep.1 = (f32[3,8,8,256]{3,2,1,0:T(8,128)}, f32[32,128]{1,0:T(8,128)}) custom-call(s32[6]{0:T(128)} %pad_add_fusion.place, s32[8]{0:T(128)} %bitcast.14, s32[8]{0:T(128)} %bitcast.15, f32[3,8,8,256]{3,2,1,0:T(8,128)} %adj_ref.5, bf16[4,3,8,8,256]{4,3,2,1,0:T(8,128)(2,1)} %st_ref.5, bf16[48,8,256]{2,1,0:T(8,128)(2,1)} %copy-done.1, ...), custom_call_target="tpu_custom_call" | custom-call | tf_op jit(solution)/shard_map/sweep/pallas_call | solution.py:269
  73.9 20.2 %all_to_all.15 = f32[32,1,128]{2,1,0:T(1,128)S(1)} all-to-all(f32[32,1,128]{2,1,0:T(1,128)} %bitcast.13), channel_id=1, replica_groups=mesh['gx_0'=4,'gx_1'=4,'gx_2'=2,'gx_3'=2,'gy'=8] {'gx_0','gx_1','gx_3'}, dimensions={0} | all-to-all | bytes 32768 | tf_op jit(solution)/shard_map/all_to_all | solution.py:300
  94.2 0.1 reduce_sum.18
  94.2 0.6 broadcast_in_dim.21
  94.8 9.1 %all-to-all-start.1 = ((f32[16,1,128]{2,1,0:T(1,128)}), f32[16,1,128]{2,1,0:T(1,128)S(1)}, u32[]{:S(2)}, u32[]{:S(2)}) async-start(f32[16,1,128]{2,1,0:T(1,128)} %broadcast_in_dim.21), calls=%async_computation.1 | async-start | bytes 16384 | tf_op jit(solution)/shard_map/all_to_all | solution.py:302
  104.0 11.2 %all-to-all-done.1 = f32[16,1,128]{2,1,0:T(1,128)S(1)} async-done(((f32[16,1,128]{2,1,0:T(1,128)}), f32[16,1,128]{2,1,0:T(1,128)S(1)}, u32[]{:S(2)}, u32[]{:S(2)}) %all-to-all-start.1) | async-done | bytes 8224 | tf_op jit(solution)/shard_map/all_to_all | solution.py:302
  115.2 0.0 copy-start.6
  115.2 0.6 copy-done.6
  115.9 0.5 fusion.1
  (2 shorter events, 0.0 us)
Async XLA Ops:
  0.6 0.7 copy-start.5
  1.9 25.2 %copy-start = (f32[256,256]{1,0:T(8,128)S(1)}, f32[256,256]{1,0:T(8,128)}, u32[]{:S(2)}) copy-start(f32[256,256]{1,0:T(8,128)} %param.11) | copy-start | bytes 786436
  3.9 23.5 %collective-permute-start = (bf16[48,8,256]{2,1,0:T(8,128)(2,1)}, bf16[48,8,256]{2,1,0:T(8,128)(2,1)S(1)}, u32[]{:S(2)}, u32[]{:S(2)}) collective-permute-start(bf16[48,8,256]{2,1,0:T(8,128)(2,1)} %get-tuple-element.8), channel_id=1, source_target_pairs={{0,504},{8,16},{16,8},{24,32},{32,24},{40,48},{48,40},{56,64},{64,... | collective-permute-start | bytes 589832 | tf_op jit(solution)/shard_map/ppermute | solution.py:244
  20.7 7.7 %collective-permute-start.1 = (bf16[48,8,256]{2,1,0:T(8,128)(2,1)}, bf16[48,8,256]{2,1,0:T(8,128)(2,1)S(1)}, u32[]{:S(2)}, u32[]{:S(2)}) collective-permute-start(bf16[48,8,256]{2,1,0:T(8,128)(2,1)} %get-tuple-element.9), channel_id=1, source_target_pairs={{0,8},{8,0},{16,24},{24,16},{32,40},{40,32},{48,56},{56,48},{64,72... | collective-permute-start | bytes 589832 | tf_op jit(solution)/shard_map/ppermute | solution.py:245
  27.4 1.0 copy-start.1
  28.4 0.7 copy-start.2
  31.4 23.2 %collective-permute-start.2 = (bf16[102,8,256]{2,1,0:T(8,128)(2,1)}, bf16[102,8,256]{2,1,0:T(8,128)(2,1)S(1)}, u32[]{:S(2)}, u32[]{:S(2)}) collective-permute-start(bf16[102,8,256]{2,1,0:T(8,128)(2,1)} %get-tuple-element.10), channel_id=1, source_target_pairs={{0,1},{1,0},{2,3},{3,2},{4,5},{5,4},{6,7},{7,6},{8,9},{9,8},{10,11... | collective-permute-start | bytes 1253384 | tf_op jit(solution)/shard_map/ppermute | solution.py:265
  42.4 22.4 %collective-permute-start.3 = (bf16[102,8,256]{2,1,0:T(8,128)(2,1)}, bf16[102,8,256]{2,1,0:T(8,128)(2,1)S(1)}, u32[]{:S(2)}, u32[]{:S(2)}) collective-permute-start(bf16[102,8,256]{2,1,0:T(8,128)(2,1)} %get-tuple-element.11), channel_id=1, source_target_pairs={{0,7},{1,2},{2,1},{3,4},{4,3},{5,6},{6,5},{7,0},{8,15},{9,10},{10,... | collective-permute-start | bytes 1253384 | tf_op jit(solution)/shard_map/ppermute | solution.py:264
  54.6 10.2 %copy-start.3 = (bf16[102,8,256]{2,1,0:T(8,128)(2,1)}, bf16[102,8,256]{2,1,0:T(8,128)(2,1)S(1)}, u32[]{:S(2)}) copy-start(bf16[102,8,256]{2,1,0:T(8,128)(2,1)S(1)} %collective-permute-done.2.even_ref) | copy-start | bytes 1253380
  64.8 0.8 copy-start.4
  94.8 20.4 %all-to-all-start.1 = ((f32[16,1,128]{2,1,0:T(1,128)}), f32[16,1,128]{2,1,0:T(1,128)S(1)}, u32[]{:S(2)}, u32[]{:S(2)}) async-start(f32[16,1,128]{2,1,0:T(1,128)} %broadcast_in_dim.21), calls=%async_computation.1 | async-start | bytes 16384 | tf_op jit(solution)/shard_map/all_to_all | solution.py:302
  115.2 0.7 copy-start.6

commit v2 on v1

v2 whole, which is shorter than its diff:
```python
import jax
import jax.numpy as jnp
from jax import lax
from jax.experimental import pallas as pl
from jax.experimental.pallas import tpu as pltpu
from jax.sharding import Mesh
from jax.sharding import PartitionSpec as P

STEPS = 4
GX = ("gx_0", "gx_1", "gx_2", "gx_3")
NEAR_AXES = ("gx_0", "gx_1", "gx_3")
FAR_AXES = ("gx_2", "gy")
TENTH = 0.2 * 0.5
LEVELS = 256
RADII = (4, 4, 3, 2, 1, 2)
REST = 5


def padded(rows):
    return (rows + 15) // 16 * 16


def enumerate_runs(lengths):
    offsets, at = {}, 0
    for key, length in lengths:
        offsets[key] = at
        at += length
    return offsets, padded(at)


EDGE_RUNS, EDGE_ROWS = enumerate_runs(
    ((f, c, d, k), r - d) for f, r in enumerate(RADII) for c in range(3) for d in range(1, r) for k in range(2)
)
CORE_RUNS, CORE_ROWS = enumerate_runs(
    ((f, c, d), 8 - 2 * (r - d)) for f, r in enumerate(RADII) for c in range(3) for d in range(1, r + 1)
)
NEAR_RUNS, NEAR_ROWS = enumerate_runs(
    ((f, c, d), 8) for f, r in enumerate(RADII) for c in range(3) for d in range(1, r + 1)
)
Y_RUNS, Y_ROWS = enumerate_runs(
    [((f, c, d), 8) for f, r in enumerate(RADII) for c in range(3) for d in range(1, r + 1)]
    + [((f, c, d, k), r - d) for f, r in enumerate(RADII) for c in range(3) for d in range(1, r) for k in range(2)]
)


def first_core():
    return lax.axis_index("gx_3") == 0


def even_slab():
    return lax.rem(lax.axis_index("gy"), 2) == 0


def own_column(steps, adj_ref, st_ref, first, field, c, p):
    x = jnp.where(first, p, 7 - p)
    if field == 0:
        return adj_ref[c, x]
    if field == REST:
        tile = adj_ref[c, x]
        return tile - tile.astype(jnp.bfloat16).astype(jnp.float32)
    return st_ref[steps[field - 1], c, x].astype(jnp.float32)


def pack_x(steps, adj_ref, st_ref, edge_ref, core_ref, near_ref, edge, core):
    first = first_core()
    for field, radius in enumerate(RADII):
        for c in range(3):
            for d in range(1, radius + 1):
                tile = own_column(steps, adj_ref, st_ref, first, field, c, d - 1)
                length = radius - d
                if length:
                    at = EDGE_RUNS[field, c, d, 0]
                    edge[at : at + length, :] = tile[:length]
                    at = EDGE_RUNS[field, c, d, 1]
                    edge[at : at + length, :] = tile[8 - length :]
                at = CORE_RUNS[field, c, d]
                core[at : at + 8 - 2 * length, :] = tile[length : 8 - length]
                at = NEAR_RUNS[field, c, d]
                near_ref[at : at + 8, :] = own_column(
                    steps, adj_ref, st_ref, first, field, c, 8 - d
                ).astype(jnp.bfloat16)
    edge_ref[...] = edge[...].astype(jnp.bfloat16)
    core_ref[...] = core[...].astype(jnp.bfloat16)


def pack_y(steps, adj_ref, st_ref, edge_ref, near_ref, odd_ref, even_ref, wide, edge, flat):
    first, even = first_core(), even_slab()
    edge[...] = edge_ref[...].astype(jnp.float32)

    def put(field, c, at, rows):
        wide[field, c, 0, at, :] = rows[:, :128]
        wide[field, c, 1, at, :] = rows[:, 128:]

    for field, radius in enumerate(RADII):
        for c in range(3):
            for p in range(8):
                at = (p + 4) * 8
                put(field, c, slice(at, at + 8), own_column(steps, adj_ref, st_ref, first, field, c, p))
            for d in range(1, radius):
                length = radius - d
                at = (4 - d) * 8
                run = EDGE_RUNS[field, c, d, 0]
                put(field, c, slice(at, at + length), edge[run : run + length, :])
                run = EDGE_RUNS[field, c, d, 1]
                put(field, c, slice(at + 8 - length, at + 8), edge[run : run + length, :])
                at, run = (11 + d) * 8, NEAR_RUNS[field, c, d]
                put(field, c, slice(at, at + 8), near_ref[run : run + 8, :].astype(jnp.float32))

    def take(field, c, run, start, length):
        at = pl.ds(start, length, stride=8)
        flat[run : run + length, 0:128] = wide[field, c, 0, at, :]
        flat[run : run + length, 128:256] = wide[field, c, 1, at, :]

    for side, out in enumerate((odd_ref, even_ref)):
        up = even if side else jnp.logical_not(even)
        for field, radius in enumerate(RADII):
            for c in range(3):
                for d in range(1, radius + 1):
                    y = jnp.where(up, 8 - d, d - 1)
                    length = radius - d
                    take(field, c, Y_RUNS[field, c, d], 4 * 8 + y, 8)
                    if length:
                        take(field, c, Y_RUNS[field, c, d, 0], (4 - length) * 8 + y, length)
                        take(field, c, Y_RUNS[field, c, d, 1], 12 * 8 + y, length)
        out[...] = flat[...].astype(jnp.bfloat16)


def rest_reach(e):
    p = e - 4
    return max(0, RADII[REST] - max(0, -p, p - 7))


def sweep(
    steps,
    tiles,
    turbines,
    adj_ref,
    st_ref,
    edge_ref,
    core_ref,
    near_ref,
    odd_ref,
    even_ref,
    whi_ref,
    wlo_ref,
    dz_ref,
    filt_ref,
    out_ref,
    part_ref,
    ext,
    solved,
    state_dz,
    kept,
    picked,
    edge,
    core,
    flat,
    wide,
):
    first, even = first_core(), even_slab()
    sign = jnp.where(first, 1.0, -1.0).astype(jnp.float32)
    edge[...] = edge_ref[...].astype(jnp.float32)
    core[...] = core_ref[...].astype(jnp.float32)
    for field, radius in enumerate(RADII):
        into = 0 if field == REST else field

        def put(c, at, rows):
            old = ext[0, c, at, :] if field == REST else 0.0
            ext[into, c, at, :] = rows + old

        for c in range(3):
            if field != REST:
                for p in range(8):
                    put(c, slice((p + 4) * 16, (p + 4) * 16 + 8), own_column(steps, adj_ref, st_ref, first, field, c, p))
            for d in range(1, radius + 1):
                at, length = (4 - d) * 16, radius - d
                if length:
                    for k, y in ((0, 0), (1, 8 - length)):
                        run = EDGE_RUNS[field, c, d, k]
                        put(c, slice(at + y, at + y + length), edge[run : run + length, :])
                run = CORE_RUNS[field, c, d]
                put(c, slice(at + length, at + 8 - length), core[run : run + 8 - 2 * length, :])
                at, run = (11 + d) * 16, NEAR_RUNS[field, c, d]
                put(c, slice(at, at + 8), near_ref[run : run + 8, :].astype(jnp.float32))

    def spread(field, c, run, start, length):
        at = pl.ds(start, length, stride=8)
        wide[field, c, 0, at, :] = flat[run : run + length, 0:128]
        wide[field, c, 1, at, :] = flat[run : run + length, 128:256]

    for side, halo in enumerate((odd_ref, even_ref)):
        up = even if side else jnp.logical_not(even)
        flat[...] = halo[...].astype(jnp.float32)
        for field, radius in enumerate(RADII):
            for c in range(3):
                for d in range(1, radius + 1):
                    y = jnp.where(up, d - 1, 8 - d)
                    length = radius - d
                    spread(field, c, Y_RUNS[field, c, d], 4 * 8 + y, 8)
                    if length:
                        spread(field, c, Y_RUNS[field, c, d, 0], (4 - length) * 8 + y, length)
                        spread(field, c, Y_RUNS[field, c, d, 1], 12 * 8 + y, length)
    for field, radius in enumerate(RADII[:REST]):
        for c in range(3):
            for e in range(5 - radius, 11 + radius):
                for half in range(2):
                    rows = wide[field, c, half, e * 8 : e * 8 + 8, :]
                    if field == 0:
                        near_rows = wide[REST, c, half, e * 8 : e * 8 + 8, :]
                        y = lax.broadcasted_iota(jnp.int32, (8, 128), 0)
                        reach = rest_reach(e)
                        if reach:
                            rows += jnp.where((y < reach) | (y >= 8 - reach), near_rows, 0.0)
                    ext[field, c, e * 16 + 8 : e * 16 + 16, half * 128 : half * 128 + 128] = rows

    for step in range(STEPS):
        reach = 3 - step
        lo, hi = 4 - reach, 12 + reach
        span = hi - lo + 2
        rows = ext[0, :, (lo - 1) * 16 : (hi + 1) * 16, :].reshape(3 * span * 16, LEVELS)
        upper = rows.astype(jnp.bfloat16)
        lower = (rows - upper.astype(jnp.float32)).astype(jnp.bfloat16)
        for half in range(2):
            lanes = slice(half * LEVELS, (half + 1) * LEVELS)
            total = jnp.dot(upper, whi_ref[:, lanes], preferred_element_type=jnp.float32)
            total += jnp.dot(lower, whi_ref[:, lanes], preferred_element_type=jnp.float32)
            total += jnp.dot(upper, wlo_ref[:, lanes], preferred_element_type=jnp.float32)
            solved[half, :, (lo - 1) * 16 : (hi + 1) * 16, :] = total.reshape(3, span * 16, LEVELS)
        field = 1 + step
        states = ext[field, :, lo * 16 : hi * 16, :].reshape(3 * (span - 2) * 16, LEVELS).astype(jnp.bfloat16)
        state_dz[:, lo * 16 : hi * 16, :] = jnp.dot(
            states, dz_ref[...], preferred_element_type=jnp.float32
        ).reshape(3, (span - 2) * 16, LEVELS)

        def one(e, carry):
            def at(ref, *lead, shift=0):
                return ref[(*lead, pl.ds(pl.multiple_of((e + shift) * 16, 16), 16), slice(None))]

            def across(ref, *lead):
                return at(ref, *lead, shift=1) - at(ref, *lead, shift=-1)

            def along(tile):
                return pltpu.roll(tile, 15, 0) - pltpu.roll(tile, 1, 0)

            sol = [at(solved, 0, c) for c in range(3)]
            vel = [at(ext, field, c) for c in range(3)]
            derivs = (
                [across(ext, field, c) for c in range(3)],
                [along(vel[c]) for c in range(3)],
                [at(state_dz, c) for c in range(3)],
            )
            stream = sign * vel[0]
            for c in range(3):
                advect = stream * across(solved, 0, c) + vel[1] * along(sol[c]) + vel[2] * at(solved, 1, c)
                couple = sol[0] * derivs[c][0] + sol[1] * derivs[c][1] + sol[2] * derivs[c][2]
                if c == 0:
                    couple = sign * couple
                ext[0, c, pl.ds(pl.multiple_of(e * 16, 16), 16), :] = sol[c] + TENTH * (advect - couple)
            return carry

        lax.fori_loop(lo, hi, one, 0)
        for p in range(8):
            kept[step, p * 8 : p * 8 + 8, :] = ext[0, 0, (p + 4) * 16 : (p + 4) * 16 + 8, :]

    for c in range(3):
        for p in range(8):
            out_ref[c, jnp.where(first, p, 7 - p)] = ext[0, c, (p + 4) * 16 : (p + 4) * 16 + 8, :]
    lane = lax.broadcasted_iota(jnp.int32, (1, 128), 1)
    total = jnp.zeros((1, 128), jnp.float32)
    for slot in range(8):
        tile = tiles[slot]
        x, y = tile // 4, 2 * lax.rem(tile, 4)
        p = jnp.where(first, x, 7 - x)
        for step in range(STEPS):
            for k in range(2):
                lanes = slice(k * LEVELS, (k + 1) * LEVELS)
                picked[slot, step : step + 1, lanes] = kept[step, pl.ds(p * 8 + y + k, 1), :]
                picked[slot, 4 + step : 5 + step, lanes] = ext[1 + step, 0, pl.ds((p + 4) * 16 + y + k, 1), :]
        both = lax.dot_general(
            picked[slot].astype(jnp.bfloat16),
            filt_ref[slot],
            (((1,), (1,)), ((), ())),
            preferred_element_type=jnp.float32,
        )
        sampled, speeds = both[0:4], both[4:8]
        term = jnp.sum(jnp.sum(speeds * speeds * sampled, axis=1, keepdims=True), axis=0, keepdims=True)
        total += jnp.where(lane == turbines[slot], term * (1.0 / 64.0), 0.0)
    part_ref[...] = jnp.broadcast_to(total, part_ref.shape)


SMEM = pl.BlockSpec(memory_space=pltpu.SMEM)
VMEM = pl.BlockSpec(memory_space=pltpu.VMEM)


def halo_rows(rows):
    return jax.ShapeDtypeStruct((rows, LEVELS), jnp.bfloat16)


def body(
    adjoint_init,
    saved_states,
    step_index,
    vertical_inverse,
    disk_filter,
    pair_turbine,
    pair_tile,
    turbine_owner,
):
    turbines = turbine_owner.shape[0]
    steps = step_index.astype(jnp.int32)
    blocks, slabs = lax.axis_size(GX), lax.axis_size("gy")
    near = [(i, i ^ 1) for i in range(blocks)]
    far = [(i, (i + 1) % blocks if i % 2 else (i - 1) % blocks) for i in range(blocks)]
    evens = [(i, i ^ 1) for i in range(slabs)]
    odds = [(i, (i + 1) % slabs if i % 2 else (i - 1) % slabs) for i in range(slabs)]

    to_edge, to_core, to_near = pl.pallas_call(
        pack_x,
        out_shape=(halo_rows(EDGE_ROWS), halo_rows(CORE_ROWS), halo_rows(NEAR_ROWS)),
        in_specs=[SMEM, VMEM, VMEM],
        out_specs=(VMEM,) * 3,
        scratch_shapes=[
            pltpu.VMEM((EDGE_ROWS, LEVELS), jnp.float32),
            pltpu.VMEM((CORE_ROWS, LEVELS), jnp.float32),
        ],
        compiler_params=pltpu.CompilerParams(vmem_limit_bytes=8 << 20),
        name="pack_x",
    )(steps, adjoint_init, saved_states)
    edge_halo = lax.ppermute(to_edge, GX, far)
    near_halo = lax.ppermute(to_near, GX, near)
    core_halo = lax.ppermute(to_core, GX, far)

    inverse_dz = jnp.pad(vertical_inverse[:, 1:], ((0, 0), (0, 1))) - jnp.pad(
        vertical_inverse[:, :-1], ((0, 0), (1, 0))
    )
    weights = jnp.concatenate([vertical_inverse, inverse_dz], axis=1)
    upper = lax.reduce_precision(weights, 8, 7)
    whi, wlo = upper.astype(jnp.bfloat16), (weights - upper).astype(jnp.bfloat16)
    k = lax.broadcasted_iota(jnp.int32, (LEVELS, LEVELS), 0)
    z = lax.broadcasted_iota(jnp.int32, (LEVELS, LEVELS), 1)
    dz = ((k == z + 1).astype(jnp.float32) - (k == z - 1).astype(jnp.float32)).astype(jnp.bfloat16)
    own_index = lax.axis_index(GX) * lax.axis_size("gy") + lax.axis_index("gy")
    mine = (turbine_owner == own_index).astype(jnp.float32)
    near_halo, whi, wlo, dz, mine = lax.optimization_barrier((near_halo, whi, wlo, dz, mine))

    to_odd, to_even = pl.pallas_call(
        pack_y,
        out_shape=(halo_rows(Y_ROWS), halo_rows(Y_ROWS)),
        in_specs=[SMEM] + [VMEM] * 4,
        out_specs=(VMEM, VMEM),
        scratch_shapes=[
            pltpu.VMEM((len(RADII), 3, 2, 128, 128), jnp.float32),
            pltpu.VMEM((EDGE_ROWS, LEVELS), jnp.float32),
            pltpu.VMEM((Y_ROWS, LEVELS), jnp.float32),
        ],
        compiler_params=pltpu.CompilerParams(vmem_limit_bytes=16 << 20),
        name="pack_y",
    )(steps, adjoint_init, saved_states, edge_halo, near_halo)
    odd_halo = lax.ppermute(to_odd, "gy", odds)
    even_halo = lax.ppermute(to_even, "gy", evens)

    close = lax.axis_size(NEAR_AXES)
    wide = lax.axis_size(FAR_AXES)
    adjoint, part = pl.pallas_call(
        sweep,
        out_shape=(
            jax.ShapeDtypeStruct(adjoint_init.shape, jnp.float32),
            jax.ShapeDtypeStruct((close, 128), jnp.float32),
        ),
        in_specs=[SMEM] * 3 + [VMEM] * 11,
        out_specs=(VMEM, VMEM),
        scratch_shapes=[
            pltpu.VMEM((5, 3, 256, LEVELS), jnp.float32),
            pltpu.VMEM((2, 3, 256, LEVELS), jnp.float32),
            pltpu.VMEM((3, 256, LEVELS), jnp.float32),
            pltpu.VMEM((STEPS, 64, LEVELS), jnp.float32),
            pltpu.VMEM((8, 8, 2 * LEVELS), jnp.float32),
            pltpu.VMEM((EDGE_ROWS, LEVELS), jnp.float32),
            pltpu.VMEM((CORE_ROWS, LEVELS), jnp.float32),
            pltpu.VMEM((Y_ROWS, LEVELS), jnp.float32),
            pltpu.VMEM((len(RADII), 3, 2, 128, 128), jnp.float32),
        ],
        compiler_params=pltpu.CompilerParams(vmem_limit_bytes=32 << 20),
        name="sweep",
    )(
        steps,
        pair_tile[0, 0],
        pair_turbine[0, 0],
        adjoint_init,
        saved_states,
        edge_halo,
        core_halo,
        near_halo,
        odd_halo,
        even_halo,
        whi,
        wlo,
        dz,
        disk_filter[0, 0],
    )
    part = jnp.sum(lax.all_to_all(part, NEAR_AXES, 0, 0, tiled=True), axis=0)
    part = jnp.broadcast_to(part[None], (wide, 128))
    totals = jnp.sum(lax.all_to_all(part, FAR_AXES, 0, 0, tiled=True), axis=0)[:turbines]
    turbine_grad = jnp.where(mine > 0.0, totals, jnp.float32(0.0))[None, None, :]
    return (adjoint, turbine_grad)


def solution(mesh):
    torus = Mesh(
        mesh.devices.reshape(4, 4, 2, 2, mesh.shape["gy"]), ("gx_0", "gx_1", "gx_2", "gx_3", "gy")
    )
    placed = (
        P(None, GX, "gy", None),
        P(None, None, GX, "gy", None),
        P(),
        P(),
        P(GX, "gy", None, None, None),
        P(GX, "gy", None),
        P(GX, "gy", None),
        P(),
    )
    return jax.shard_map(
        body,
        mesh=torus,
        in_specs=placed,
        out_specs=(P(None, GX, "gy", None), P(GX, "gy", None)),
        check_vma=False,
    )
```

time: 117 us -> 109 us (0.932)
  blocking collectives: 20.2 us -> 44.1 us
  starting transfers between devices: 53.9 us -> 36.5 us
  waiting for transfers between devices: 22.4 us -> 12.5 us
  Pallas kernels: 12.7 us -> 8.98 us
  other arithmetic: 2.93 us -> 0.85 us
  local copies, waits for them, and re-layouts: 3.45 us -> 4.94 us
    all_to_all x0 -> x1, blocking collectives: none -> 19 us  [body(): lax.all_to_all(part, FAR_AXES, 0, 0, tiled=True)]
    ppermute x1 -> x2, waiting for transfers between devices: 0.01 us -> 12.5 us  [the longest x1 12.5 us: body(): core_halo = lax.ppermute(to_core, GX, far)]
    all_to_all x1 -> x0, waiting for transfers between devices: 11.2 us -> none  [body(): lax.all_to_all(part, FAR_AXES, 0, 0, tiled=True)]
    ppermute x1, waiting for transfers between devices: 10.2 us -> 0.01 us  [body(): odd_halo = lax.ppermute(to_odd, 'gy', odds)]
    all_to_all x1 -> x0, starting transfers between devices: 9.13 us -> none  [body(): lax.all_to_all(part, FAR_AXES, 0, 0, tiled=True)]
    ppermute x1, starting transfers between devices: 11 us -> 1.92 us  [body(): even_halo = lax.ppermute(to_even, 'gy', evens)]
    ppermute x1 -> x2, starting transfers between devices: 16.8 us -> 22.8 us  [the longest x1 16.8 us: body(): edge_halo = lax.ppermute(to_edge, GX, far)]
    ppermute x1, starting transfers between devices: 10.6 us -> 5.38 us  [body(): odd_halo = lax.ppermute(to_odd, 'gy', odds)]
  transfers between devices with their start and end apart: 5 -> 5, of which waited for: 3 -> 1; matrix products, arithmetic and copies ran while one was open for 2% -> 0% of each run, Pallas kernels for 0% -> 0%
where the time goes in v2:
time: 109 us
  blocking collectives  44.1 us (40%)
  starting transfers between devices  36.5 us (33%)
  waiting for transfers between devices  12.5 us (11%)
  Pallas kernels  8.98 us (8%)
  local copies, waits for them, and re-layouts  4.94 us (5%)
    all_to_all x1, blocking collectives, body(): part = jnp.sum(lax.all_to_all(part, NEAR_AXES, 0, 0, tiled=True), axis=0)  25 us
    all_to_all x1, blocking collectives, body(): lax.all_to_all(part, FAR_AXES, 0, 0, tiled=True)  19 us
    ppermute x1, starting transfers between devices, body(): edge_halo = lax.ppermute(to_edge, GX, far)  16.8 us
    ppermute x1, waiting for transfers between devices, body(): core_halo = lax.ppermute(to_core, GX, far)  12.5 us
    pallas_call x1, Pallas kernels, body(): pl.pallas_call(sweep, out_shape=(jax.ShapeDtypeStruct(adjoint_init.shape,...  7.33 us
    ppermute x1, starting transfers between devices, body(): near_halo = lax.ppermute(to_near, GX, near)  6.39 us
    ppermute x1, starting transfers between devices, body(): core_halo = lax.ppermute(to_core, GX, far)  6.01 us
    ppermute x1, starting transfers between devices, body(): odd_halo = lax.ppermute(to_odd, 'gy', odds)  5.38 us
  transfers between devices with their start and end apart: 5, of which 1 were waited for; matrix products, arithmetic and copies ran while one was open for 0% of the time, Pallas kernels for 0%

profile of v2, /device:TPU:1, one launch (start us, length us, event | category | flops | bytes accessed | tf_op | source)
XLA Modules:
  0.0 108.7 jit_solution(11141697340993790083)
XLA Ops:
  0.6 0.0 copy-start
  0.6 1.0 copy-done
  1.6 0.0 copy-start.2
  1.6 0.9 copy-done.2
  2.6 0.0 copy-start.5
  2.6 0.7 copy-done.5
  3.2 0.0 copy-start.9
  3.2 0.6 pack_x.1
  3.9 16.8 %collective-permute-start = (bf16[112,256]{1,0:T(8,128)(2,1)S(1)}, bf16[112,256]{1,0:T(8,128)(2,1)S(1)}, u32[]{:S(2)}, u32[]{:S(2)}) collective-permute-start(bf16[112,256]{1,0:T(8,128)(2,1)S(1)} %get-tuple-element.14), channel_id=1, source_target_pairs={{0,504},{8,16},{16,8},{24,32},{32,24},{40,48},{48,40},{56,64},{64,... | collective-permute-start | bytes 172040 | tf_op jit(solution)/shard_map/ppermute | solution.py:329
  20.7 6.4 %collective-permute-start.2 = (bf16[384,256]{1,0:T(8,128)(2,1)S(1)}, bf16[384,256]{1,0:T(8,128)(2,1)S(1)}, u32[]{:S(2)}, u32[]{:S(2)}) collective-permute-start(bf16[384,256]{1,0:T(8,128)(2,1)S(1)} %get-tuple-element.16), channel_id=1, source_target_pairs={{0,8},{8,0},{16,24},{24,16},{32,40},{40,32},{48,56},{56,48},{64,72... | collective-permute-start | bytes 589832 | tf_op jit(solution)/shard_map/ppermute | solution.py:330
  27.1 0.0 copy-done.9
  27.1 0.1 fusion.2
  27.3 0.0 copy-start.10
  27.3 0.6 copy-done.10
  27.9 0.1 subtract_convert_fusion.dz_ref
  28.0 0.1 pad_subtract_fusion
  28.1 0.0 copy-start.1
  28.2 0.0 copy-start.3
  28.2 0.0 copy-start.6
  28.2 0.1 fusion
  28.3 0.0 copy-start.4
  28.3 0.0 collective-permute-done.2.near_ref
  28.3 0.0 collective-permute-done.edge_ref
  28.3 0.9 copy-done.1
  29.1 0.0 copy-done.3
  29.2 0.0 copy-done.6
  29.2 1.0 pack_y.1
  30.2 5.4 %collective-permute-start.3 = (bf16[496,256]{1,0:T(8,128)(2,1)S(1)}, bf16[496,256]{1,0:T(8,128)(2,1)S(1)}, u32[]{:S(2)}, u32[]{:S(2)}) collective-permute-start(bf16[496,256]{1,0:T(8,128)(2,1)S(1)} %get-tuple-element.18), channel_id=1, source_target_pairs={{0,7},{1,2},{2,1},{3,4},{4,3},{5,6},{6,5},{7,0},{8,15},{9,10},{10,... | collective-permute-start | bytes 761864 | tf_op jit(solution)/shard_map/ppermute | solution.py:359
  35.6 1.9 %collective-permute-start.4 = (bf16[496,256]{1,0:T(8,128)(2,1)S(1)}, bf16[496,256]{1,0:T(8,128)(2,1)S(1)}, u32[]{:S(2)}, u32[]{:S(2)}) collective-permute-start(bf16[496,256]{1,0:T(8,128)(2,1)S(1)} %get-tuple-element.19), channel_id=1, source_target_pairs={{0,1},{1,0},{2,3},{3,2},{4,5},{5,4},{6,7},{7,6},{8,9},{9,8},{10,11... | collective-permute-start | bytes 761864 | tf_op jit(solution)/shard_map/ppermute | solution.py:360
  37.5 6.0 %collective-permute-start.1 = (bf16[288,256]{1,0:T(8,128)(2,1)S(1)}, bf16[288,256]{1,0:T(8,128)(2,1)S(1)}, u32[]{:S(2)}, u32[]{:S(2)}) collective-permute-start(bf16[288,256]{1,0:T(8,128)(2,1)S(1)} %get-tuple-element.15), channel_id=1, source_target_pairs={{0,504},{8,16},{16,8},{24,32},{32,24},{40,48},{48,40},{56,64},{64,... | collective-permute-start | bytes 442376 | tf_op jit(solution)/shard_map/ppermute | solution.py:331
  43.5 12.5 %collective-permute-done.1.core_ref = bf16[288,256]{1,0:T(8,128)(2,1)S(1)} collective-permute-done((bf16[288,256]{1,0:T(8,128)(2,1)S(1)}, bf16[288,256]{1,0:T(8,128)(2,1)S(1)}, u32[]{:S(2)}, u32[]{:S(2)}) %collective-permute-start.1) | collective-permute-done | bytes 147488 | tf_op jit(solution)/shard_map/ppermute | solution.py:331
  56.0 0.0 collective-permute-done.3.odd_ref
  56.0 0.0 collective-permute-done.4.even_ref
  56.0 0.0 copy-start.7
  56.0 0.0 copy-start.8
  56.0 0.0 copy-done.4
  56.1 0.6 copy-done.7
  56.7 0.0 copy-done.8
  56.7 7.3 %sweep.1 = (f32[3,8,8,256]{3,2,1,0:T(8,128)}, f32[32,128]{1,0:T(8,128)S(1)}) custom-call(s32[4]{0:T(128)S(1)} %copy-done.6, s32[8]{0:T(128)S(1)} %bitcast.11, s32[8]{0:T(128)S(1)} %bitcast.12, f32[3,8,8,256]{3,2,1,0:T(8,128)S(1)} %copy-done.3, bf16[4,3,8,8,256]{4,3,2,1,0:T(8,128)(2,1)S(1)} %copy-done.1, bf16[112,256]{1,0:T(8,128)(2,1)S(1)} %collective-permute-done.edge_ref, ...), custom_call_target="tpu_custom_call" | custom-call | tf_op jit(solution)/shard_map/sweep/pallas_call | solution.py:364
  64.0 25.0 %all_to_all.15 = f32[32,1,128]{2,1,0:T(1,128)S(1)} all-to-all(f32[32,1,128]{2,1,0:T(1,128)S(1)} %bitcast.10), channel_id=1, replica_groups=mesh['gx_0'=4,'gx_1'=4,'gx_2'=2,'gx_3'=2,'gy'=8] {'gx_0','gx_1','gx_3'}, dimensions={0} | all-to-all | bytes 32768 | tf_op jit(solution)/shard_map/all_to_all | solution.py:401
  89.1 0.1 reduce_sum.18
  89.1 19.0 %all_to_all.16 = f32[16,1,128]{2,1,0:T(1,128)S(1)} all-to-all(f32[16,1,128]{2,1,0:T(1,128)S(1)} %broadcast_in_dim.6), channel_id=1, replica_groups=mesh['gx_0'=4,'gx_1'=4,'gx_2'=2,'gx_3'=2,'gy'=8] {'gx_2','gy'}, dimensions={0} | all-to-all | bytes 16384 | tf_op jit(solution)/shard_map/all_to_all | solution.py:403
  108.2 0.5 fusion.1
  (4 shorter events, 0.0 us)
Async XLA Ops:
  0.6 1.0 copy-start
  1.6 0.9 copy-start.2
  2.6 0.7 copy-start.5
  3.2 23.9 %copy-start.9 = (f32[256,256]{1,0:T(8,128)S(1)}, f32[256,256]{1,0:T(8,128)}, u32[]{:S(2)}) copy-start(f32[256,256]{1,0:T(8,128)} %param.11) | copy-start | bytes 786436
  3.9 24.4 %collective-permute-start = (bf16[112,256]{1,0:T(8,128)(2,1)S(1)}, bf16[112,256]{1,0:T(8,128)(2,1)S(1)}, u32[]{:S(2)}, u32[]{:S(2)}) collective-permute-start(bf16[112,256]{1,0:T(8,128)(2,1)S(1)} %get-tuple-element.14), channel_id=1, source_target_pairs={{0,504},{8,16},{16,8},{24,32},{32,24},{40,48},{48,40},{56,64},{64,... | collective-permute-start | bytes 172040 | tf_op jit(solution)/shard_map/ppermute | solution.py:329
  20.7 7.6 %collective-permute-start.2 = (bf16[384,256]{1,0:T(8,128)(2,1)S(1)}, bf16[384,256]{1,0:T(8,128)(2,1)S(1)}, u32[]{:S(2)}, u32[]{:S(2)}) collective-permute-start(bf16[384,256]{1,0:T(8,128)(2,1)S(1)} %get-tuple-element.16), channel_id=1, source_target_pairs={{0,8},{8,0},{16,24},{24,16},{32,40},{40,32},{48,56},{56,48},{64,72... | collective-permute-start | bytes 589832 | tf_op jit(solution)/shard_map/ppermute | solution.py:330
  27.3 0.7 copy-start.10
  28.1 1.0 copy-start.1
  28.2 1.0 copy-start.3
  28.2 1.0 copy-start.6
  28.3 27.8 %copy-start.4 = (bf16[1,1,8,64,512]{4,3,2,1,0:T(8,128)(2,1)S(1)}, bf16[1,1,8,64,512]{4,3,2,1,0:T(8,128)(2,1)}, u32[]{:S(2)}) copy-start(bf16[1,1,8,64,512]{4,3,2,1,0:T(8,128)(2,1)} %param.12) | copy-start | bytes 1572868
  30.2 25.8 %collective-permute-start.3 = (bf16[496,256]{1,0:T(8,128)(2,1)S(1)}, bf16[496,256]{1,0:T(8,128)(2,1)S(1)}, u32[]{:S(2)}, u32[]{:S(2)}) collective-permute-start(bf16[496,256]{1,0:T(8,128)(2,1)S(1)} %get-tuple-element.18), channel_id=1, source_target_pairs={{0,7},{1,2},{2,1},{3,4},{4,3},{5,6},{6,5},{7,0},{8,15},{9,10},{10,... | collective-permute-start | bytes 761864 | tf_op jit(solution)/shard_map/ppermute | solution.py:359
  35.6 20.4 %collective-permute-start.4 = (bf16[496,256]{1,0:T(8,128)(2,1)S(1)}, bf16[496,256]{1,0:T(8,128)(2,1)S(1)}, u32[]{:S(2)}, u32[]{:S(2)}) collective-permute-start(bf16[496,256]{1,0:T(8,128)(2,1)S(1)} %get-tuple-element.19), channel_id=1, source_target_pairs={{0,1},{1,0},{2,3},{3,2},{4,5},{5,4},{6,7},{7,6},{8,9},{9,8},{10,11... | collective-permute-start | bytes 761864 | tf_op jit(solution)/shard_map/ppermute | solution.py:360
  37.5 18.5 %collective-permute-start.1 = (bf16[288,256]{1,0:T(8,128)(2,1)S(1)}, bf16[288,256]{1,0:T(8,128)(2,1)S(1)}, u32[]{:S(2)}, u32[]{:S(2)}) collective-permute-start(bf16[288,256]{1,0:T(8,128)(2,1)S(1)} %get-tuple-element.15), channel_id=1, source_target_pairs={{0,504},{8,16},{16,8},{24,32},{32,24},{40,48},{48,40},{56,64},{64,... | collective-permute-start | bytes 442376 | tf_op jit(solution)/shard_map/ppermute | solution.py:331
  56.0 0.7 copy-start.7
  56.0 0.7 copy-start.8

commit v3 on v2

--- a/solution.py
+++ b/solution.py
@@ -12,7 +12,7 @@
 FAR_AXES = ("gx_2", "gy")
 TENTH = 0.2 * 0.5
 LEVELS = 256
-RADII = (4, 4, 3, 2, 1, 2)
+RADII = (4, 4, 3, 2, 1, 1)
 REST = 5
 
 
@@ -61,12 +61,21 @@
     return st_ref[steps[field - 1], c, x].astype(jnp.float32)
 
 
-def pack_x(steps, adj_ref, st_ref, edge_ref, core_ref, near_ref, edge, core):
+def pack_x(steps_ref, adj_ref, st_ref, edge_ref, core_ref, near_ref, edge, core, steps, adj, st, sems):
     first = first_core()
+    copies = (
+        pltpu.make_async_copy(steps_ref, steps, sems.at[0]),
+        pltpu.make_async_copy(adj_ref, adj, sems.at[1]),
+        pltpu.make_async_copy(st_ref, st, sems.at[2]),
+    )
+    for copy in copies:
+        copy.start()
+    for copy in copies:
+        copy.wait()
     for field, radius in enumerate(RADII):
         for c in range(3):
             for d in range(1, radius + 1):
-                tile = own_column(steps, adj_ref, st_ref, first, field, c, d - 1)
+                tile = own_column(steps, adj, st, first, field, c, d - 1)
                 length = radius - d
                 if length:
                     at = EDGE_RUNS[field, c, d, 0]
@@ -76,9 +85,7 @@
                 at = CORE_RUNS[field, c, d]
                 core[at : at + 8 - 2 * length, :] = tile[length : 8 - length]
                 at = NEAR_RUNS[field, c, d]
-                near_ref[at : at + 8, :] = own_column(
-                    steps, adj_ref, st_ref, first, field, c, 8 - d
-                ).astype(jnp.bfloat16)
+                near_ref[at : at + 8, :] = own_column(steps, adj, st, first, field, c, 8 - d).astype(jnp.bfloat16)
     edge_ref[...] = edge[...].astype(jnp.bfloat16)
     core_ref[...] = core[...].astype(jnp.bfloat16)
 
@@ -125,6 +132,25 @@
         out[...] = flat[...].astype(jnp.bfloat16)
 
 
+def prepare(inverse_ref, owner_ref, filt_ref, weights_ref, dz_ref, mine_ref, staged_ref):
+    inverse = inverse_ref[...]
+    k = lax.broadcasted_iota(jnp.int32, (LEVELS, LEVELS), 0)
+    z = lax.broadcasted_iota(jnp.int32, (LEVELS, LEVELS), 1)
+    above = jnp.where(z < LEVELS - 1, pltpu.roll(inverse, LEVELS - 1, 1), 0.0)
+    below = jnp.where(z > 0, pltpu.roll(inverse, 1, 1), 0.0)
+    for half, weights in enumerate((inverse, above - below)):
+        lanes = slice(half * LEVELS, (half + 1) * LEVELS)
+        upper = weights.astype(jnp.bfloat16)
+        weights_ref[0:LEVELS, lanes] = upper
+        weights_ref[LEVELS : 2 * LEVELS, lanes] = upper
+        weights_ref[2 * LEVELS :, lanes] = (weights - upper.astype(jnp.float32)).astype(jnp.bfloat16)
+    dz = (k == z + 1).astype(jnp.float32) - (k == z - 1).astype(jnp.float32)
+    dz_ref[...] = dz.astype(jnp.bfloat16)
+    own_index = lax.axis_index(GX) * lax.axis_size("gy") + lax.axis_index("gy")
+    mine_ref[...] = (owner_ref[...] == own_index).astype(jnp.float32)
+    staged_ref[...] = filt_ref[...]
+
+
 def rest_reach(e):
     p = e - 4
     return max(0, RADII[REST] - max(0, -p, p - 7))
@@ -132,8 +158,7 @@
 
 def sweep(
     steps,
-    tiles,
-    turbines,
+    slots,
     adj_ref,
     st_ref,
     edge_ref,
@@ -141,8 +166,7 @@
     near_ref,
     odd_ref,
     even_ref,
-    whi_ref,
-    wlo_ref,
+    weights_ref,
     dz_ref,
     filt_ref,
     out_ref,
@@ -220,11 +244,10 @@
         rows = ext[0, :, (lo - 1) * 16 : (hi + 1) * 16, :].reshape(3 * span * 16, LEVELS)
         upper = rows.astype(jnp.bfloat16)
         lower = (rows - upper.astype(jnp.float32)).astype(jnp.bfloat16)
+        stacked = jnp.concatenate([upper, lower, upper], axis=1)
         for half in range(2):
             lanes = slice(half * LEVELS, (half + 1) * LEVELS)
-            total = jnp.dot(upper, whi_ref[:, lanes], preferred_element_type=jnp.float32)
-            total += jnp.dot(lower, whi_ref[:, lanes], preferred_element_type=jnp.float32)
-            total += jnp.dot(upper, wlo_ref[:, lanes], preferred_element_type=jnp.float32)
+            total = jnp.dot(stacked, weights_ref[:, lanes], preferred_element_type=jnp.float32)
             solved[half, :, (lo - 1) * 16 : (hi + 1) * 16, :] = total.reshape(3, span * 16, LEVELS)
         field = 1 + step
         states = ext[field, :, lo * 16 : hi * 16, :].reshape(3 * (span - 2) * 16, LEVELS).astype(jnp.bfloat16)
@@ -258,7 +281,7 @@
                 ext[0, c, pl.ds(pl.multiple_of(e * 16, 16), 16), :] = sol[c] + TENTH * (advect - couple)
             return carry
 
-        lax.fori_loop(lo, hi, one, 0)
+        lax.fori_loop(lo, hi, one, 0, unroll=2)
         for p in range(8):
             kept[step, p * 8 : p * 8 + 8, :] = ext[0, 0, (p + 4) * 16 : (p + 4) * 16 + 8, :]
 
@@ -268,7 +291,7 @@
     lane = lax.broadcasted_iota(jnp.int32, (1, 128), 1)
     total = jnp.zeros((1, 128), jnp.float32)
     for slot in range(8):
-        tile = tiles[slot]
+        tile = slots[slot]
         x, y = tile // 4, 2 * lax.rem(tile, 4)
         p = jnp.where(first, x, 7 - x)
         for step in range(STEPS):
@@ -284,7 +307,7 @@
         )
         sampled, speeds = both[0:4], both[4:8]
         term = jnp.sum(jnp.sum(speeds * speeds * sampled, axis=1, keepdims=True), axis=0, keepdims=True)
-        total += jnp.where(lane == turbines[slot], term * (1.0 / 64.0), 0.0)
+        total += jnp.where(lane == slots[8 + slot], term * (1.0 / 64.0), 0.0)
     part_ref[...] = jnp.broadcast_to(total, part_ref.shape)
 
 
@@ -317,31 +340,37 @@
     to_edge, to_core, to_near = pl.pallas_call(
         pack_x,
         out_shape=(halo_rows(EDGE_ROWS), halo_rows(CORE_ROWS), halo_rows(NEAR_ROWS)),
-        in_specs=[SMEM, VMEM, VMEM],
+        in_specs=[pl.BlockSpec(memory_space=pl.ANY)] * 3,
         out_specs=(VMEM,) * 3,
         scratch_shapes=[
             pltpu.VMEM((EDGE_ROWS, LEVELS), jnp.float32),
             pltpu.VMEM((CORE_ROWS, LEVELS), jnp.float32),
+            pltpu.SMEM((STEPS,), jnp.int32),
+            pltpu.VMEM(adjoint_init.shape, jnp.float32),
+            pltpu.VMEM(saved_states.shape, jnp.bfloat16),
+            pltpu.SemaphoreType.DMA((3,)),
         ],
-        compiler_params=pltpu.CompilerParams(vmem_limit_bytes=8 << 20),
+        compiler_params=pltpu.CompilerParams(vmem_limit_bytes=67043328),
         name="pack_x",
     )(steps, adjoint_init, saved_states)
     edge_halo = lax.ppermute(to_edge, GX, far)
     near_halo = lax.ppermute(to_near, GX, near)
     core_halo = lax.ppermute(to_core, GX, far)
 
-    inverse_dz = jnp.pad(vertical_inverse[:, 1:], ((0, 0), (0, 1))) - jnp.pad(
-        vertical_inverse[:, :-1], ((0, 0), (1, 0))
-    )
-    weights = jnp.concatenate([vertical_inverse, inverse_dz], axis=1)
-    upper = lax.reduce_precision(weights, 8, 7)
-    whi, wlo = upper.astype(jnp.bfloat16), (weights - upper).astype(jnp.bfloat16)
-    k = lax.broadcasted_iota(jnp.int32, (LEVELS, LEVELS), 0)
-    z = lax.broadcasted_iota(jnp.int32, (LEVELS, LEVELS), 1)
-    dz = ((k == z + 1).astype(jnp.float32) - (k == z - 1).astype(jnp.float32)).astype(jnp.bfloat16)
-    own_index = lax.axis_index(GX) * lax.axis_size("gy") + lax.axis_index("gy")
-    mine = (turbine_owner == own_index).astype(jnp.float32)
-    near_halo, whi, wlo, dz, mine = lax.optimization_barrier((near_halo, whi, wlo, dz, mine))
+    filters = disk_filter[0, 0]
+    weights, dz, mine, filters = pl.pallas_call(
+        prepare,
+        out_shape=(
+            jax.ShapeDtypeStruct((3 * LEVELS, 2 * LEVELS), jnp.bfloat16),
+            jax.ShapeDtypeStruct((LEVELS, LEVELS), jnp.bfloat16),
+            jax.ShapeDtypeStruct((1, turbines), jnp.float32),
+            jax.ShapeDtypeStruct(filters.shape, jnp.bfloat16),
+        ),
+        in_specs=[VMEM] * 3,
+        out_specs=(VMEM,) * 4,
+        compiler_params=pltpu.CompilerParams(vmem_limit_bytes=4 << 20),
+        name="prepare",
+    )(vertical_inverse, turbine_owner[None], filters)
 
     to_odd, to_even = pl.pallas_call(
         pack_y,
@@ -359,6 +388,8 @@
     odd_halo = lax.ppermute(to_odd, "gy", odds)
     even_halo = lax.ppermute(to_even, "gy", evens)
 
+    slots = jnp.concatenate([pair_tile[0, 0], pair_turbine[0, 0]])
+    odd_halo, slots = lax.optimization_barrier((odd_halo, slots))
     close = lax.axis_size(NEAR_AXES)
     wide = lax.axis_size(FAR_AXES)
     adjoint, part = pl.pallas_call(
@@ -367,7 +398,7 @@
             jax.ShapeDtypeStruct(adjoint_init.shape, jnp.float32),
             jax.ShapeDtypeStruct((close, 128), jnp.float32),
         ),
-        in_specs=[SMEM] * 3 + [VMEM] * 11,
+        in_specs=[SMEM] * 2 + [VMEM] * 10,
         out_specs=(VMEM, VMEM),
         scratch_shapes=[
             pltpu.VMEM((5, 3, 256, LEVELS), jnp.float32),
@@ -384,8 +415,7 @@
         name="sweep",
     )(
         steps,
-        pair_tile[0, 0],
-        pair_turbine[0, 0],
+        slots,
         adjoint_init,
         saved_states,
         edge_halo,
@@ -393,15 +423,14 @@
         near_halo,
         odd_halo,
         even_halo,
-        whi,
-        wlo,
+        weights,
         dz,
-        disk_filter[0, 0],
+        filters,
     )
     part = jnp.sum(lax.all_to_all(part, NEAR_AXES, 0, 0, tiled=True), axis=0)
     part = jnp.broadcast_to(part[None], (wide, 128))
     totals = jnp.sum(lax.all_to_all(part, FAR_AXES, 0, 0, tiled=True), axis=0)[:turbines]
-    turbine_grad = jnp.where(mine > 0.0, totals, jnp.float32(0.0))[None, None, :]
+    turbine_grad = jnp.where(mine[0] > 0.0, totals, jnp.float32(0.0))[None, None, :]
     return (adjoint, turbine_grad)
 
 

time: 109 us -> 108 us (level)
  waiting for transfers between devices: 12.5 us -> 15.1 us
  blocking collectives: 44.1 us -> 41.7 us
  local copies, waits for them, and re-layouts: 4.94 us -> 3.24 us
  Pallas kernels: 8.98 us -> 10.3 us
    all_to_all x1, blocking collectives: 25 us -> 17.8 us  [body(): part = jnp.sum(lax.all_to_all(part, NEAR_AXES, 0, 0, tiled=True), axis=0)]
    ppermute x1, starting transfers between devices: 16.8 us -> 9.99 us  [body(): edge_halo = lax.ppermute(to_edge, GX, far)]
    all_to_all x1, blocking collectives: 19 us -> 23.9 us  [body(): lax.all_to_all(part, FAR_AXES, 0, 0, tiled=True)]
    ppermute x1, waiting for transfers between devices: 0.01 us -> 4.43 us  [body(): edge_halo = lax.ppermute(to_edge, GX, far)]
    ppermute x1, starting transfers between devices: 6.39 us -> 8.75 us  [body(): near_halo = lax.ppermute(to_near, GX, near)]
    ppermute x1, starting transfers between devices: 5.38 us -> 7.71 us  [body(): odd_halo = lax.ppermute(to_odd, 'gy', odds)]
    ppermute x1, starting transfers between devices: 6.01 us -> 7.84 us  [body(): core_halo = lax.ppermute(to_core, GX, far)]
    ppermute x1, waiting for transfers between devices: 12.5 us -> 10.7 us  [body(): core_halo = lax.ppermute(to_core, GX, far)]
  transfers between devices with their start and end apart: 5 -> 5, of which waited for: 1 -> 2; matrix products, arithmetic and copies ran while one was open for 0% -> 0% of each run, Pallas kernels for 0% -> 0%
where the time goes in v3:
time: 108 us
  blocking collectives  41.7 us (39%)
  starting transfers between devices  36.2 us (34%)
  waiting for transfers between devices  15.1 us (14%)
  Pallas kernels  10.3 us (10%)
  local copies, waits for them, and re-layouts  3.24 us (3%)
    all_to_all x1, blocking collectives, body(): lax.all_to_all(part, FAR_AXES, 0, 0, tiled=True)  23.9 us
    all_to_all x1, blocking collectives, body(): part = jnp.sum(lax.all_to_all(part, NEAR_AXES, 0, 0, tiled=True), axis=0)  17.8 us
    ppermute x1, waiting for transfers between devices, body(): core_halo = lax.ppermute(to_core, GX, far)  10.7 us
    ppermute x1, starting transfers between devices, body(): edge_halo = lax.ppermute(to_edge, GX, far)  9.99 us
    ppermute x1, starting transfers between devices, body(): near_halo = lax.ppermute(to_near, GX, near)  8.75 us
    ppermute x1, starting transfers between devices, body(): core_halo = lax.ppermute(to_core, GX, far)  7.84 us
    ppermute x1, starting transfers between devices, body(): odd_halo = lax.ppermute(to_odd, 'gy', odds)  7.71 us
    pallas_call x1, Pallas kernels, body(): pl.pallas_call(sweep, out_shape=(jax.ShapeDtypeStruct(adjoint_init.shape,...  7.15 us
  transfers between devices with their start and end apart: 5, of which 2 were waited for; matrix products, arithmetic and copies ran while one was open for 0% of the time, Pallas kernels for 0%

profile of v3, /device:TPU:1, one launch (start us, length us, event | category | flops | bytes accessed | tf_op | source)
XLA Modules:
  0.0 108.0 jit_solution(2654013815029721095)
XLA Ops:
  0.6 1.9 %pack_x.1 = (bf16[96,256]{1,0:T(8,128)(2,1)}, bf16[272,256]{1,0:T(8,128)(2,1)}, bf16[368,256]{1,0:T(8,128)(2,1)}) custom-call(s32[4]{0:T(128)} %steps.3, f32[3,8,8,256]{3,2,1,0:T(8,128)} %adj_ref.5, bf16[4,3,8,8,256]{4,3,2,1,0:T(8,128)(2,1)} %st_ref.5), custom_call_target="tpu_custom_call" | custom-call | tf_op jit(solution)/shard_map/pack_x/pallas_call | solution.py:340
  2.6 0.0 copy-start.6
  2.6 8.7 %collective-permute-start.1 = (bf16[368,256]{1,0:T(8,128)(2,1)}, bf16[368,256]{1,0:T(8,128)(2,1)S(1)}, u32[]{:S(2)}, u32[]{:S(2)}) collective-permute-start(bf16[368,256]{1,0:T(8,128)(2,1)} %get-tuple-element.16), channel_id=1, source_target_pairs={{0,8},{8,0},{16,24},{24,16},{32,40},{40,32},{48,56},{56,48},{64,72... | collective-permute-start | bytes 565256 | tf_op jit(solution)/shard_map/ppermute | solution.py:357
  11.3 10.0 %collective-permute-start = (bf16[96,256]{1,0:T(8,128)(2,1)}, bf16[96,256]{1,0:T(8,128)(2,1)S(1)}, u32[]{:S(2)}, u32[]{:S(2)}) collective-permute-start(bf16[96,256]{1,0:T(8,128)(2,1)} %get-tuple-element.15), channel_id=1, source_target_pairs={{0,504},{8,16},{16,8},{24,32},{32,24},{40,48},{48,40},{56,64},{64,... | collective-permute-start | bytes 147464 | tf_op jit(solution)/shard_map/ppermute | solution.py:356
  21.3 4.4 %collective-permute-done.edge_ref = bf16[96,256]{1,0:T(8,128)(2,1)S(1)} collective-permute-done((bf16[96,256]{1,0:T(8,128)(2,1)}, bf16[96,256]{1,0:T(8,128)(2,1)S(1)}, u32[]{:S(2)}, u32[]{:S(2)}) %collective-permute-start) | collective-permute-done | bytes 49184 | tf_op jit(solution)/shard_map/ppermute | solution.py:356
  25.8 0.0 collective-permute-done.1.near_ref
  25.8 0.0 copy-done.6
  25.8 0.0 copy-start
  25.8 1.0 copy-done
  26.8 0.0 copy-start.2
  26.8 0.9 copy-done.2
  27.7 0.0 copy-start.4
  27.7 0.0 copy-start.5
  27.7 1.0 pack_y.1
  28.7 7.7 %collective-permute-start.2 = (bf16[464,256]{1,0:T(8,128)(2,1)S(1)}, bf16[464,256]{1,0:T(8,128)(2,1)S(1)}, u32[]{:S(2)}, u32[]{:S(2)}) collective-permute-start(bf16[464,256]{1,0:T(8,128)(2,1)S(1)} %get-tuple-element.17), channel_id=1, source_target_pairs={{0,7},{1,2},{2,1},{3,4},{4,3},{5,6},{6,5},{7,0},{8,15},{9,10},{10,... | collective-permute-start | bytes 712712 | tf_op jit(solution)/shard_map/ppermute | solution.py:388
  36.4 1.9 %collective-permute-start.4 = (bf16[464,256]{1,0:T(8,128)(2,1)S(1)}, bf16[464,256]{1,0:T(8,128)(2,1)S(1)}, u32[]{:S(2)}, u32[]{:S(2)}) collective-permute-start(bf16[464,256]{1,0:T(8,128)(2,1)S(1)} %get-tuple-element.21), channel_id=1, source_target_pairs={{0,1},{1,0},{2,3},{3,2},{4,5},{5,4},{6,7},{7,6},{8,9},{9,8},{10,11... | collective-permute-start | bytes 712712 | tf_op jit(solution)/shard_map/ppermute | solution.py:389
  38.3 7.8 %collective-permute-start.3 = (bf16[272,256]{1,0:T(8,128)(2,1)}, bf16[272,256]{1,0:T(8,128)(2,1)S(1)}, u32[]{:S(2)}, u32[]{:S(2)}) collective-permute-start(bf16[272,256]{1,0:T(8,128)(2,1)} %get-tuple-element.19), channel_id=1, source_target_pairs={{0,504},{8,16},{16,8},{24,32},{32,24},{40,48},{48,40},{56,64},{64,... | collective-permute-start | bytes 417800 | tf_op jit(solution)/shard_map/ppermute | solution.py:358
  46.2 0.0 copy-start.7
  46.2 0.0 copy-done.4
  46.2 0.0 copy-done.5
  46.2 0.6 copy-done.7
  46.8 0.0 copy-start.1
  46.8 0.0 copy-start.3
  46.8 0.3 prepare.1
  47.1 0.0 copy-start.8
  47.1 0.0 copy-start.9
  47.1 0.6 copy-done.8
  47.8 0.0 copy-done.9
  47.8 0.1 pad_add_fusion.slots
  47.9 0.0 collective-permute-done.2.odd_ref
  47.9 10.7 %collective-permute-done.3.core_ref = bf16[272,256]{1,0:T(8,128)(2,1)S(1)} collective-permute-done((bf16[272,256]{1,0:T(8,128)(2,1)}, bf16[272,256]{1,0:T(8,128)(2,1)S(1)}, u32[]{:S(2)}, u32[]{:S(2)}) %collective-permute-start.3) | collective-permute-done | bytes 139296 | tf_op jit(solution)/shard_map/ppermute | solution.py:358
  58.6 0.0 collective-permute-done.4.even_ref
  58.6 0.0 copy-done.1
  58.6 0.0 copy-done.3
  58.6 7.1 %sweep.1 = (f32[3,8,8,256]{3,2,1,0:T(8,128)}, f32[32,128]{1,0:T(8,128)S(1)}) custom-call(s32[4]{0:T(128)S(1)} %copy-done.6, s32[16]{0:T(128)S(1)} %pad_add_fusion.slots, f32[3,8,8,256]{3,2,1,0:T(8,128)S(1)} %copy-done.3, bf16[4,3,8,8,256]{4,3,2,1,0:T(8,128)(2,1)S(1)} %copy-done.1, bf16[96,256]{1,0:T(8,128)(2,1)S(1)} %collective-permute-done.edge_ref, ...), custom_call_target="tpu_custom_call" | custom-call | tf_op jit(solution)/shard_map/sweep/pallas_call | solution.py:395
  65.7 17.8 %all_to_all.15 = f32[32,1,128]{2,1,0:T(1,128)S(1)} all-to-all(f32[32,1,128]{2,1,0:T(1,128)S(1)} %bitcast.15), channel_id=1, replica_groups=mesh['gx_0'=4,'gx_1'=4,'gx_2'=2,'gx_3'=2,'gy'=8] {'gx_0','gx_1','gx_3'}, dimensions={0} | all-to-all | bytes 32768 | tf_op jit(solution)/shard_map/all_to_all | solution.py:430
  83.5 0.1 reduce_sum.18
  83.6 23.9 %all_to_all.16 = f32[16,1,128]{2,1,0:T(1,128)S(1)} all-to-all(f32[16,1,128]{2,1,0:T(1,128)S(1)} %broadcast_in_dim.15), channel_id=1, replica_groups=mesh['gx_0'=4,'gx_1'=4,'gx_2'=2,'gx_3'=2,'gy'=8] {'gx_2','gy'}, dimensions={0} | all-to-all | bytes 16384 | tf_op jit(solution)/shard_map/all_to_all | solution.py:432
  107.5 0.5 fusion
  (2 shorter events, 0.0 us)
Async XLA Ops:
  2.6 23.2 %copy-start.6 = (s32[4]{0:T(128)S(1)}, s32[4]{0:T(128)}, u32[]{:S(2)}) copy-start(s32[4]{0:T(128)} %steps.3) | copy-start | bytes 52
  2.6 23.2 %collective-permute-start.1 = (bf16[368,256]{1,0:T(8,128)(2,1)}, bf16[368,256]{1,0:T(8,128)(2,1)S(1)}, u32[]{:S(2)}, u32[]{:S(2)}) collective-permute-start(bf16[368,256]{1,0:T(8,128)(2,1)} %get-tuple-element.16), channel_id=1, source_target_pairs={{0,8},{8,0},{16,24},{24,16},{32,40},{40,32},{48,56},{56,48},{64,72... | collective-permute-start | bytes 565256 | tf_op jit(solution)/shard_map/ppermute | solution.py:357
  11.3 14.4 %collective-permute-start = (bf16[96,256]{1,0:T(8,128)(2,1)}, bf16[96,256]{1,0:T(8,128)(2,1)S(1)}, u32[]{:S(2)}, u32[]{:S(2)}) collective-permute-start(bf16[96,256]{1,0:T(8,128)(2,1)} %get-tuple-element.15), channel_id=1, source_target_pairs={{0,504},{8,16},{16,8},{24,32},{32,24},{40,48},{48,40},{56,64},{64,... | collective-permute-start | bytes 147464 | tf_op jit(solution)/shard_map/ppermute | solution.py:356
  25.8 1.0 copy-start
  26.8 0.9 copy-start.2
  27.7 18.5 %copy-start.4 = (bf16[1,1,8,64,512]{4,3,2,1,0:T(8,128)(2,1)S(1)}, bf16[1,1,8,64,512]{4,3,2,1,0:T(8,128)(2,1)}, u32[]{:S(2)}) copy-start(bf16[1,1,8,64,512]{4,3,2,1,0:T(8,128)(2,1)} %param.12) | copy-start | bytes 1572868
  27.7 18.5 %copy-start.5 = (f32[256,256]{1,0:T(8,128)S(1)}, f32[256,256]{1,0:T(8,128)}, u32[]{:S(2)}) copy-start(f32[256,256]{1,0:T(8,128)} %inverse_ref.1) | copy-start | bytes 786436
  28.7 19.2 %collective-permute-start.2 = (bf16[464,256]{1,0:T(8,128)(2,1)S(1)}, bf16[464,256]{1,0:T(8,128)(2,1)S(1)}, u32[]{:S(2)}, u32[]{:S(2)}) collective-permute-start(bf16[464,256]{1,0:T(8,128)(2,1)S(1)} %get-tuple-element.17), channel_id=1, source_target_pairs={{0,7},{1,2},{2,1},{3,4},{4,3},{5,6},{6,5},{7,0},{8,15},{9,10},{10,... | collective-permute-start | bytes 712712 | tf_op jit(solution)/shard_map/ppermute | solution.py:388
  36.4 22.2 %collective-permute-start.4 = (bf16[464,256]{1,0:T(8,128)(2,1)S(1)}, bf16[464,256]{1,0:T(8,128)(2,1)S(1)}, u32[]{:S(2)}, u32[]{:S(2)}) collective-permute-start(bf16[464,256]{1,0:T(8,128)(2,1)S(1)} %get-tuple-element.21), channel_id=1, source_target_pairs={{0,1},{1,0},{2,3},{3,2},{4,5},{5,4},{6,7},{7,6},{8,9},{9,8},{10,11... | collective-permute-start | bytes 712712 | tf_op jit(solution)/shard_map/ppermute | solution.py:389
  38.3 20.2 %collective-permute-start.3 = (bf16[272,256]{1,0:T(8,128)(2,1)}, bf16[272,256]{1,0:T(8,128)(2,1)S(1)}, u32[]{:S(2)}, u32[]{:S(2)}) collective-permute-start(bf16[272,256]{1,0:T(8,128)(2,1)} %get-tuple-element.19), channel_id=1, source_target_pairs={{0,504},{8,16},{16,8},{24,32},{32,24},{40,48},{48,40},{56,64},{64,... | collective-permute-start | bytes 417800 | tf_op jit(solution)/shard_map/ppermute | solution.py:358
  46.2 0.7 copy-start.7
  46.8 11.7 %copy-start.1 = (bf16[4,3,8,8,256]{4,3,2,1,0:T(8,128)(2,1)S(1)}, bf16[4,3,8,8,256]{4,3,2,1,0:T(8,128)(2,1)}, u32[]{:S(2)}) copy-start(bf16[4,3,8,8,256]{4,3,2,1,0:T(8,128)(2,1)} %st_ref.5) | copy-start | bytes 1179652
  46.8 11.7 %copy-start.3 = (f32[3,8,8,256]{3,2,1,0:T(8,128)S(1)}, f32[3,8,8,256]{3,2,1,0:T(8,128)}, u32[]{:S(2)}) copy-start(f32[3,8,8,256]{3,2,1,0:T(8,128)} %adj_ref.5) | copy-start | bytes 589828
  47.1 0.7 copy-start.8
  47.1 0.7 copy-start.9

commit v4 on v3

--- a/solution.py
+++ b/solution.py
@@ -272,16 +272,19 @@
                 [along(vel[c]) for c in range(3)],
                 [at(state_dz, c) for c in range(3)],
             )
+            keep = 8 if step == STEPS - 1 else 16
             stream = sign * vel[0]
             for c in range(3):
                 advect = stream * across(solved, 0, c) + vel[1] * along(sol[c]) + vel[2] * at(solved, 1, c)
                 couple = sol[0] * derivs[c][0] + sol[1] * derivs[c][1] + sol[2] * derivs[c][2]
                 if c == 0:
                     couple = sign * couple
-                ext[0, c, pl.ds(pl.multiple_of(e * 16, 16), 16), :] = sol[c] + TENTH * (advect - couple)
+                ext[0, c, pl.ds(pl.multiple_of(e * 16, 16), keep), :] = (
+                    sol[c][:keep] + TENTH * (advect[:keep] - couple[:keep])
+                )
             return carry
 
-        lax.fori_loop(lo, hi, one, 0, unroll=2)
+        lax.fori_loop(lo, hi, one, 0, unroll=(2, 4, 2, 4)[step])
         for p in range(8):
             kept[step, p * 8 : p * 8 + 8, :] = ext[0, 0, (p + 4) * 16 : (p + 4) * 16 + 8, :]
 

time: 108 us -> 108 us (level)
  no operation moved by 1% of the time
where the time goes in v4:
time: 108 us
  blocking collectives  41.7 us (39%)
  starting transfers between devices  36.2 us (34%)
  waiting for transfers between devices  15.1 us (14%)
  Pallas kernels  10.2 us (9%)
  local copies, waits for them, and re-layouts  3.24 us (3%)
    all_to_all x1, blocking collectives, body(): lax.all_to_all(part, FAR_AXES, 0, 0, tiled=True)  23.9 us
    all_to_all x1, blocking collectives, body(): part = jnp.sum(lax.all_to_all(part, NEAR_AXES, 0, 0, tiled=True), axis=0)  17.8 us
    ppermute x1, waiting for transfers between devices, body(): core_halo = lax.ppermute(to_core, GX, far)  10.7 us
    ppermute x1, starting transfers between devices, body(): edge_halo = lax.ppermute(to_edge, GX, far)  9.99 us
    ppermute x1, starting transfers between devices, body(): near_halo = lax.ppermute(to_near, GX, near)  8.75 us
    ppermute x1, starting transfers between devices, body(): core_halo = lax.ppermute(to_core, GX, far)  7.84 us
    ppermute x1, starting transfers between devices, body(): odd_halo = lax.ppermute(to_odd, 'gy', odds)  7.71 us
    pallas_call x1, Pallas kernels, body(): pl.pallas_call(sweep, out_shape=(jax.ShapeDtypeStruct(adjoint_init.shape,...  6.97 us
  transfers between devices with their start and end apart: 5, of which 2 were waited for; matrix products, arithmetic and copies ran while one was open for 0% of the time, Pallas kernels for 0%

profile of v4, /device:TPU:1, one launch (start us, length us, event | category | flops | bytes accessed | tf_op | source)
XLA Modules:
  0.0 107.8 jit_solution(17622802897653255110)
XLA Ops:
  0.6 1.9 %pack_x.1 = (bf16[96,256]{1,0:T(8,128)(2,1)}, bf16[272,256]{1,0:T(8,128)(2,1)}, bf16[368,256]{1,0:T(8,128)(2,1)}) custom-call(s32[4]{0:T(128)} %steps.3, f32[3,8,8,256]{3,2,1,0:T(8,128)} %adj_ref.5, bf16[4,3,8,8,256]{4,3,2,1,0:T(8,128)(2,1)} %st_ref.5), custom_call_target="tpu_custom_call" | custom-call | tf_op jit(solution)/shard_map/pack_x/pallas_call | solution.py:343
  2.6 0.0 copy-start.6
  2.6 8.7 %collective-permute-start.1 = (bf16[368,256]{1,0:T(8,128)(2,1)}, bf16[368,256]{1,0:T(8,128)(2,1)S(1)}, u32[]{:S(2)}, u32[]{:S(2)}) collective-permute-start(bf16[368,256]{1,0:T(8,128)(2,1)} %get-tuple-element.16), channel_id=1, source_target_pairs={{0,8},{8,0},{16,24},{24,16},{32,40},{40,32},{48,56},{56,48},{64,72... | collective-permute-start | bytes 565256 | tf_op jit(solution)/shard_map/ppermute | solution.py:360
  11.3 10.0 %collective-permute-start = (bf16[96,256]{1,0:T(8,128)(2,1)}, bf16[96,256]{1,0:T(8,128)(2,1)S(1)}, u32[]{:S(2)}, u32[]{:S(2)}) collective-permute-start(bf16[96,256]{1,0:T(8,128)(2,1)} %get-tuple-element.15), channel_id=1, source_target_pairs={{0,504},{8,16},{16,8},{24,32},{32,24},{40,48},{48,40},{56,64},{64,... | collective-permute-start | bytes 147464 | tf_op jit(solution)/shard_map/ppermute | solution.py:359
  21.3 4.4 %collective-permute-done.edge_ref = bf16[96,256]{1,0:T(8,128)(2,1)S(1)} collective-permute-done((bf16[96,256]{1,0:T(8,128)(2,1)}, bf16[96,256]{1,0:T(8,128)(2,1)S(1)}, u32[]{:S(2)}, u32[]{:S(2)}) %collective-permute-start) | collective-permute-done | bytes 49184 | tf_op jit(solution)/shard_map/ppermute | solution.py:359
  25.8 0.0 collective-permute-done.1.near_ref
  25.8 0.0 copy-done.6
  25.8 0.0 copy-start
  25.8 1.0 copy-done
  26.8 0.0 copy-start.2
  26.8 0.9 copy-done.2
  27.7 0.0 copy-start.4
  27.7 0.0 copy-start.5
  27.7 1.0 pack_y.1
  28.7 7.7 %collective-permute-start.2 = (bf16[464,256]{1,0:T(8,128)(2,1)S(1)}, bf16[464,256]{1,0:T(8,128)(2,1)S(1)}, u32[]{:S(2)}, u32[]{:S(2)}) collective-permute-start(bf16[464,256]{1,0:T(8,128)(2,1)S(1)} %get-tuple-element.17), channel_id=1, source_target_pairs={{0,7},{1,2},{2,1},{3,4},{4,3},{5,6},{6,5},{7,0},{8,15},{9,10},{10,... | collective-permute-start | bytes 712712 | tf_op jit(solution)/shard_map/ppermute | solution.py:391
  36.4 1.9 %collective-permute-start.4 = (bf16[464,256]{1,0:T(8,128)(2,1)S(1)}, bf16[464,256]{1,0:T(8,128)(2,1)S(1)}, u32[]{:S(2)}, u32[]{:S(2)}) collective-permute-start(bf16[464,256]{1,0:T(8,128)(2,1)S(1)} %get-tuple-element.21), channel_id=1, source_target_pairs={{0,1},{1,0},{2,3},{3,2},{4,5},{5,4},{6,7},{7,6},{8,9},{9,8},{10,11... | collective-permute-start | bytes 712712 | tf_op jit(solution)/shard_map/ppermute | solution.py:392
  38.3 7.8 %collective-permute-start.3 = (bf16[272,256]{1,0:T(8,128)(2,1)}, bf16[272,256]{1,0:T(8,128)(2,1)S(1)}, u32[]{:S(2)}, u32[]{:S(2)}) collective-permute-start(bf16[272,256]{1,0:T(8,128)(2,1)} %get-tuple-element.19), channel_id=1, source_target_pairs={{0,504},{8,16},{16,8},{24,32},{32,24},{40,48},{48,40},{56,64},{64,... | collective-permute-start | bytes 417800 | tf_op jit(solution)/shard_map/ppermute | solution.py:361
  46.2 0.0 copy-start.7
  46.2 0.0 copy-done.4
  46.2 0.0 copy-done.5
  46.2 0.6 copy-done.7
  46.8 0.0 copy-start.1
  46.8 0.0 copy-start.3
  46.8 0.3 prepare.1
  47.1 0.0 copy-start.8
  47.1 0.0 copy-start.9
  47.1 0.6 copy-done.8
  47.8 0.0 copy-done.9
  47.8 0.1 pad_add_fusion.slots
  47.9 0.0 collective-permute-done.2.odd_ref
  47.9 10.7 %collective-permute-done.3.core_ref = bf16[272,256]{1,0:T(8,128)(2,1)S(1)} collective-permute-done((bf16[272,256]{1,0:T(8,128)(2,1)}, bf16[272,256]{1,0:T(8,128)(2,1)S(1)}, u32[]{:S(2)}, u32[]{:S(2)}) %collective-permute-start.3) | collective-permute-done | bytes 139296 | tf_op jit(solution)/shard_map/ppermute | solution.py:361
  58.6 0.0 collective-permute-done.4.even_ref
  58.6 0.0 copy-done.1
  58.6 0.0 copy-done.3
  58.6 7.0 %sweep.1 = (f32[3,8,8,256]{3,2,1,0:T(8,128)}, f32[32,128]{1,0:T(8,128)S(1)}) custom-call(s32[4]{0:T(128)S(1)} %copy-done.6, s32[16]{0:T(128)S(1)} %pad_add_fusion.slots, f32[3,8,8,256]{3,2,1,0:T(8,128)S(1)} %copy-done.3, bf16[4,3,8,8,256]{4,3,2,1,0:T(8,128)(2,1)S(1)} %copy-done.1, bf16[96,256]{1,0:T(8,128)(2,1)S(1)} %collective-permute-done.edge_ref, ...), custom_call_target="tpu_custom_call" | custom-call | tf_op jit(solution)/shard_map/sweep/pallas_call | solution.py:398
  65.5 17.8 %all_to_all.15 = f32[32,1,128]{2,1,0:T(1,128)S(1)} all-to-all(f32[32,1,128]{2,1,0:T(1,128)S(1)} %bitcast.15), channel_id=1, replica_groups=mesh['gx_0'=4,'gx_1'=4,'gx_2'=2,'gx_3'=2,'gy'=8] {'gx_0','gx_1','gx_3'}, dimensions={0} | all-to-all | bytes 32768 | tf_op jit(solution)/shard_map/all_to_all | solution.py:433
  83.3 0.1 reduce_sum.18
  83.4 23.9 %all_to_all.16 = f32[16,1,128]{2,1,0:T(1,128)S(1)} all-to-all(f32[16,1,128]{2,1,0:T(1,128)S(1)} %broadcast_in_dim.15), channel_id=1, replica_groups=mesh['gx_0'=4,'gx_1'=4,'gx_2'=2,'gx_3'=2,'gy'=8] {'gx_2','gy'}, dimensions={0} | all-to-all | bytes 16384 | tf_op jit(solution)/shard_map/all_to_all | solution.py:435
  107.3 0.5 fusion
  (2 shorter events, 0.0 us)
Async XLA Ops:
  2.6 23.2 %copy-start.6 = (s32[4]{0:T(128)S(1)}, s32[4]{0:T(128)}, u32[]{:S(2)}) copy-start(s32[4]{0:T(128)} %steps.3) | copy-start | bytes 52
  2.6 23.2 %collective-permute-start.1 = (bf16[368,256]{1,0:T(8,128)(2,1)}, bf16[368,256]{1,0:T(8,128)(2,1)S(1)}, u32[]{:S(2)}, u32[]{:S(2)}) collective-permute-start(bf16[368,256]{1,0:T(8,128)(2,1)} %get-tuple-element.16), channel_id=1, source_target_pairs={{0,8},{8,0},{16,24},{24,16},{32,40},{40,32},{48,56},{56,48},{64,72... | collective-permute-start | bytes 565256 | tf_op jit(solution)/shard_map/ppermute | solution.py:360
  11.3 14.4 %collective-permute-start = (bf16[96,256]{1,0:T(8,128)(2,1)}, bf16[96,256]{1,0:T(8,128)(2,1)S(1)}, u32[]{:S(2)}, u32[]{:S(2)}) collective-permute-start(bf16[96,256]{1,0:T(8,128)(2,1)} %get-tuple-element.15), channel_id=1, source_target_pairs={{0,504},{8,16},{16,8},{24,32},{32,24},{40,48},{48,40},{56,64},{64,... | collective-permute-start | bytes 147464 | tf_op jit(solution)/shard_map/ppermute | solution.py:359
  25.8 1.0 copy-start
  26.8 0.9 copy-start.2
  27.7 18.5 %copy-start.4 = (bf16[1,1,8,64,512]{4,3,2,1,0:T(8,128)(2,1)S(1)}, bf16[1,1,8,64,512]{4,3,2,1,0:T(8,128)(2,1)}, u32[]{:S(2)}) copy-start(bf16[1,1,8,64,512]{4,3,2,1,0:T(8,128)(2,1)} %param.12) | copy-start | bytes 1572868
  27.7 18.5 %copy-start.5 = (f32[256,256]{1,0:T(8,128)S(1)}, f32[256,256]{1,0:T(8,128)}, u32[]{:S(2)}) copy-start(f32[256,256]{1,0:T(8,128)} %inverse_ref.1) | copy-start | bytes 786436
  28.7 19.2 %collective-permute-start.2 = (bf16[464,256]{1,0:T(8,128)(2,1)S(1)}, bf16[464,256]{1,0:T(8,128)(2,1)S(1)}, u32[]{:S(2)}, u32[]{:S(2)}) collective-permute-start(bf16[464,256]{1,0:T(8,128)(2,1)S(1)} %get-tuple-element.17), channel_id=1, source_target_pairs={{0,7},{1,2},{2,1},{3,4},{4,3},{5,6},{6,5},{7,0},{8,15},{9,10},{10,... | collective-permute-start | bytes 712712 | tf_op jit(solution)/shard_map/ppermute | solution.py:391
  36.4 22.2 %collective-permute-start.4 = (bf16[464,256]{1,0:T(8,128)(2,1)S(1)}, bf16[464,256]{1,0:T(8,128)(2,1)S(1)}, u32[]{:S(2)}, u32[]{:S(2)}) collective-permute-start(bf16[464,256]{1,0:T(8,128)(2,1)S(1)} %get-tuple-element.21), channel_id=1, source_target_pairs={{0,1},{1,0},{2,3},{3,2},{4,5},{5,4},{6,7},{7,6},{8,9},{9,8},{10,11... | collective-permute-start | bytes 712712 | tf_op jit(solution)/shard_map/ppermute | solution.py:392
  38.3 20.2 %collective-permute-start.3 = (bf16[272,256]{1,0:T(8,128)(2,1)}, bf16[272,256]{1,0:T(8,128)(2,1)S(1)}, u32[]{:S(2)}, u32[]{:S(2)}) collective-permute-start(bf16[272,256]{1,0:T(8,128)(2,1)} %get-tuple-element.19), channel_id=1, source_target_pairs={{0,504},{8,16},{16,8},{24,32},{32,24},{40,48},{48,40},{56,64},{64,... | collective-permute-start | bytes 417800 | tf_op jit(solution)/shard_map/ppermute | solution.py:361
  46.2 0.7 copy-start.7
  46.8 11.7 %copy-start.1 = (bf16[4,3,8,8,256]{4,3,2,1,0:T(8,128)(2,1)S(1)}, bf16[4,3,8,8,256]{4,3,2,1,0:T(8,128)(2,1)}, u32[]{:S(2)}) copy-start(bf16[4,3,8,8,256]{4,3,2,1,0:T(8,128)(2,1)} %st_ref.5) | copy-start | bytes 1179652
  46.8 11.7 %copy-start.3 = (f32[3,8,8,256]{3,2,1,0:T(8,128)S(1)}, f32[3,8,8,256]{3,2,1,0:T(8,128)}, u32[]{:S(2)}) copy-start(f32[3,8,8,256]{3,2,1,0:T(8,128)} %adj_ref.5) | copy-start | bytes 589828
  47.1 0.7 copy-start.8
  47.1 0.7 copy-start.9
